TPU v7x, 32 devices: a whole 2x2x4 slice. The times are simulated.
32 devices in a mesh: seq: 32 (over z, y, x, core).
Axes of the slice: x: 2, y: 2, z: 4, core: 2. Of those that a mesh axis runs over, the one named last changes fastest.
Arguments:
- tokens: bfloat16 [4, 2048, 768], P(None, 'seq'), may hold values from -6 to 6
- doc_lengths: int32 [4, 16], replicated, may hold values from 1 to 512, 2048 in all within a row
- first_gain: float32 [768], replicated, may hold values from 0.5 to 1.5
- first_shift: float32 [768], replicated, may hold values from -1.75 to 1.75
- input_weight: bfloat16 [768, 2304], replicated, may hold values from -0.21875 to 0.21875
- input_bias: float32 [2304], replicated, may hold values from -1.75 to 1.75
- short_kernel: float32 [3, 2304], replicated, may hold values from -3.5 to 3.5
- short_bias: float32 [2304], replicated, may hold values from -1.75 to 1.75
- embed_weight: float32 [33, 64], replicated, may hold values from -2 to 2
- embed_bias: float32 [64], replicated, may hold values from -3.140625 to 3.140625
- inner_weight: float32 [64, 64], replicated, may hold values from -1.5 to 1.5
- inner_bias: float32 [64], replicated, may hold values from -3.140625 to 3.140625
- filter_weight: float32 [64, 768], replicated, may hold values from -0.03125 to 0.03125
- decay_rates: float32 [768], replicated, may hold values from 3.07 to 15.35
- filter_bias: float32 [768], replicated, may hold values from -3 to 3
- output_weight: bfloat16 [768, 768], replicated, may hold values from -0.21875 to 0.21875
- output_bias: float32 [768], replicated, may hold values from -1.75 to 1.75
- second_gain: float32 [768], replicated, may hold values from 0.5 to 1.5
- second_shift: float32 [768], replicated, may hold values from -1.75 to 1.75
- up_weight: bfloat16 [768, 3072], replicated, may hold values from -0.21875 to 0.21875
- up_bias: float32 [3072], replicated, may hold values from -1.75 to 1.75
- down_weight: bfloat16 [3072, 768], replicated, may hold values from -0.109375 to 0.109375
- down_bias: float32 [768], replicated, may hold values from -1.75 to 1.75
- cotangent: bfloat16 [4, 2048, 768], P(None, 'seq'), may hold values from -6 to 6
Outputs:
- output: bfloat16 [4, 2048, 768], P(None, 'seq')
- grad_tokens: bfloat16 [4, 2048, 768], P(None, 'seq')
- grad_first_gain: float32 [768], replicated
- grad_first_shift: float32 [768], replicated
- grad_input_weight: float32 [768, 2304], replicated
- grad_input_bias: float32 [2304], replicated
- grad_short_kernel: float32 [3, 2304], replicated
- grad_short_bias: float32 [2304], replicated
- grad_embed_weight: float32 [33, 64], replicated
- grad_embed_bias: float32 [64], replicated
- grad_inner_weight: float32 [64, 64], replicated
- grad_inner_bias: float32 [64], replicated
- grad_filter_weight: float32 [64, 768], replicated
- grad_decay_rates: float32 [768], replicated
- grad_filter_bias: float32 [768], replicated
- grad_output_weight: float32 [768, 768], replicated
- grad_output_bias: float32 [768], replicated
- grad_second_gain: float32 [768], replicated
- grad_second_shift: float32 [768], replicated
- grad_up_weight: float32 [768, 3072], replicated
- grad_up_bias: float32 [3072], replicated
- grad_down_weight: float32 [3072, 768], replicated
- grad_down_bias: float32 [768], replicated
Inputs may be any that keep to these rules, and one draw needn't show every extreme that they name: `doc_lengths`: the lengths of one sequence add up to 2048, and the longest document of each sequence has exactly 512 positions.
All inputs are finite; a program needn't handle non-finite values.
Results may differ from a plain program's by a relative error of at most 0.014.
Values may be sent and summed in bfloat16 or wider, within the bound.
A program may use at most 192 MiB of HBM per device.

v0:
```python
import functools
import math

import jax
import jax.numpy as jnp
from jax import lax
from jax.sharding import PartitionSpec as P

HIGHEST_PRECISION = lax.Precision.HIGHEST
EPSILON = 1e-05


def from_behind(block, axis, distance):
    devices = range(lax.axis_size(axis))
    route = [(i - distance, i) for i in devices if i - distance in devices]
    return lax.ppermute(block, axis, route)


def shortened(x):
    return jax.tree.map(lambda a: a.astype(jnp.bfloat16) if a.dtype == jnp.float32 else a, x)


def layer_norm(values, norm_gain, norm_shift):
    center = values - jnp.mean(values, axis=-1, keepdims=True)
    spread = jnp.mean(center * center, axis=-1, keepdims=True)
    return center * lax.rsqrt(spread + EPSILON) * norm_gain + norm_shift


def embed_positions(positions, length, embed_width):
    band_count = (embed_width - 1) // 2
    harmonic = jnp.arange(1, band_count + 1, dtype=jnp.int32)
    phases = positions[:, None] * harmonic[None, :] % length
    angles = 2.0 * math.pi / length * phases.astype(jnp.float32)
    scaled = positions.astype(jnp.float32)[:, None] / length
    return jnp.concatenate([scaled, jnp.cos(angles), jnp.sin(angles)], axis=1)


def build_filter(
    embed_weight,
    embed_bias,
    inner_weight,
    inner_bias,
    filter_weight,
    decay_rates,
    embedded=None,
    scaled_positions=None,
):
    first_hidden = jnp.sin(
        jnp.dot(embedded, embed_weight, precision=HIGHEST_PRECISION) + embed_bias
    )
    second_hidden = jnp.sin(
        jnp.dot(first_hidden, inner_weight, precision=HIGHEST_PRECISION) + inner_bias
    )
    raw_filter = jnp.dot(second_hidden, filter_weight, precision=HIGHEST_PRECISION)
    return raw_filter * jnp.exp(-decay_rates[None, :] * scaled_positions[:, None])


def dft_tables(half_count, column_count):
    full_count = 2 * half_count
    total_count = full_count * column_count
    first_rows = jnp.arange(half_count, dtype=jnp.int32)
    first_freqs = jnp.arange(full_count, dtype=jnp.int32)
    second_index = jnp.arange(column_count, dtype=jnp.int32)
    first_angles = (
        2.0
        * math.pi
        / full_count
        * (first_rows[:, None] * first_freqs[None, :] % full_count).astype(jnp.float32)
    )
    second_angles = (
        2.0
        * math.pi
        / column_count
        * (second_index[:, None] * second_index[None, :] % column_count).astype(jnp.float32)
    )
    twist_angles = (
        2.0
        * math.pi
        / total_count
        * (first_freqs[:, None] * second_index[None, :] % total_count).astype(jnp.float32)
    )
    return (
        jnp.cos(first_angles),
        jnp.sin(first_angles),
        jnp.cos(second_angles),
        jnp.sin(second_angles),
        jnp.cos(twist_angles)[:, :, None],
        jnp.sin(twist_angles)[:, :, None],
    )


def first_section(values, matrix):
    return jnp.einsum("...nbc,nk->...kbc", values, matrix, precision=HIGHEST_PRECISION)


def first_back(values, matrix):
    return jnp.einsum("...kbc,nk->...nbc", values, matrix, precision=HIGHEST_PRECISION)


def second_section(values, matrix):
    return jnp.einsum("...kbc,bj->...kjc", values, matrix, precision=HIGHEST_PRECISION)


def second_back(values, matrix):
    return jnp.einsum("...kjc,bj->...kbc", values, matrix, precision=HIGHEST_PRECISION)


def forward_spectrum(values, tables):
    first_cos, first_sin, second_cos, second_sin, twist_cos, twist_sin = tables
    half_count = first_cos.shape[0]
    column_count = second_cos.shape[0]
    shaped = values.reshape(values.shape[:-2] + (half_count, column_count, values.shape[-1]))
    real_one = first_section(shaped, first_cos)
    imag_one = -first_section(shaped, first_sin)
    real_two = real_one * twist_cos + imag_one * twist_sin
    imag_two = imag_one * twist_cos - real_one * twist_sin
    real_out = second_section(real_two, second_cos) + second_section(imag_two, second_sin)
    imag_out = second_section(imag_two, second_cos) - second_section(real_two, second_sin)
    return (real_out, imag_out)


def inverse_half(real_in, imag_in, tables):
    first_cos, first_sin, second_cos, second_sin, twist_cos, twist_sin = tables
    half_count = first_cos.shape[0]
    column_count = second_cos.shape[0]
    real_one = second_back(real_in, second_cos) - second_back(imag_in, second_sin)
    imag_one = second_back(imag_in, second_cos) + second_back(real_in, second_sin)
    real_two = real_one * twist_cos - imag_one * twist_sin
    imag_two = imag_one * twist_cos + real_one * twist_sin
    result = first_back(real_two, first_cos) - first_back(imag_two, first_sin)
    result = result * (1.0 / (2 * half_count * column_count))
    return result.reshape(result.shape[:-3] + (half_count * column_count, result.shape[-1]))


def shards(
    tokens,
    doc_lengths,
    first_gain,
    first_shift,
    input_weight,
    input_bias,
    short_kernel,
    short_bias,
    embed_weight,
    embed_bias,
    inner_weight,
    inner_bias,
    filter_weight,
    decay_rates,
    filter_bias,
    output_weight,
    output_bias,
    second_gain,
    second_shift,
    up_weight,
    up_bias,
    down_weight,
    down_bias,
    cotangent,
):
    row_count, local_count, model_width = tokens.shape
    stream_width = 3 * model_width
    device_count = lax.axis_size("seq")
    seq_length = local_count * device_count
    offset = lax.axis_index("seq") * local_count
    positions = offset + jnp.arange(local_count, dtype=jnp.int32)
    doc_ends = jnp.cumsum(doc_lengths, axis=1)[:, :-1]
    starting = jnp.any(positions[None, :, None] == doc_ends[:, None, :], axis=-1) | (
        positions[None, :] == 0
    )
    keep_one = jnp.where(starting, 0.0, 1.0).astype(jnp.float32)
    keep_two = keep_one * jnp.concatenate(
        [jnp.ones((row_count, 1), jnp.float32), keep_one[:, :-1]], axis=1
    )
    keep_one_col = keep_one[:, :, None]
    keep_two_col = keep_two[:, :, None]
    token_values = tokens.astype(jnp.float32)
    first_norm, first_pullback = jax.vjp(layer_norm, token_values, first_gain, first_shift)
    normed = first_norm.astype(jnp.bfloat16)
    projected = (
        jnp.einsum("rsd,de->rse", normed, input_weight, preferred_element_type=jnp.float32)
        + input_bias
    ).astype(jnp.bfloat16)
    rim_rows = jnp.concatenate(
        [projected[:, -2:-1] * keep_one_col[:, -1:].astype(jnp.bfloat16), projected[:, -1:]], axis=1
    )
    previous = from_behind(rim_rows, "seq", 1)
    extended = jnp.concatenate([previous, projected], axis=1).astype(jnp.float32)
    lag_one = extended[:, 1:-1]
    lag_two = extended[:, :-2]
    proj_values = extended[:, 2:]
    short_out = (
        short_kernel[0] * proj_values
        + short_kernel[1] * keep_one_col * lag_one
        + short_kernel[2] * keep_two_col * lag_two
        + short_bias
    )
    gate_zero = short_out[..., :model_width]
    gate_one = short_out[..., model_width : 2 * model_width]
    value_part = short_out[..., 2 * model_width :]
    gated = value_part * gate_one
    tables = dft_tables(local_count, device_count)
    embedded = embed_positions(positions, seq_length, embed_weight.shape[0])
    scaled_positions = positions.astype(jnp.float32) / seq_length
    filter_fn = functools.partial(
        build_filter, embedded=embedded, scaled_positions=scaled_positions
    )
    filter_rows, filter_pullback = jax.vjp(
        filter_fn, embed_weight, embed_bias, inner_weight, inner_bias, filter_weight, decay_rates
    )
    spread_gated, spread_filter = (
        lax.all_to_all(
            gated.astype(jnp.bfloat16), "seq", split_axis=2, concat_axis=1, tiled=True
        ).astype(gated.dtype),
        lax.all_to_all(
            filter_rows[None].astype(jnp.bfloat16), "seq", split_axis=2, concat_axis=1, tiled=True
        ).astype(jnp.float32),
    )
    spread_filter = spread_filter[0]
    gated_real, gated_imag = forward_spectrum(spread_gated, tables)
    filter_real, filter_imag = forward_spectrum(spread_filter[None], tables)
    conv_real = gated_real * filter_real - gated_imag * filter_imag
    conv_imag = gated_real * filter_imag + gated_imag * filter_real
    conv_columns = inverse_half(conv_real, conv_imag, tables)
    conv_rows = lax.all_to_all(
        shortened(conv_columns), "seq", split_axis=1, concat_axis=2, tiled=True
    ).astype(conv_columns.dtype)
    conv_full = conv_rows + filter_bias * gated
    mixed_low = (conv_full * gate_zero).astype(jnp.bfloat16)
    branch = (
        jnp.einsum("rsd,de->rse", mixed_low, output_weight, preferred_element_type=jnp.float32)
        + output_bias
    )
    residual = token_values + branch
    second_norm, second_pullback = jax.vjp(layer_norm, residual, second_gain, second_shift)
    normed_two = second_norm.astype(jnp.bfloat16)
    pre_active = (
        jnp.einsum("rsd,df->rsf", normed_two, up_weight, preferred_element_type=jnp.float32)
        + up_bias
    )
    activated, gelu_pullback = jax.vjp(functools.partial(jax.nn.gelu, approximate=True), pre_active)
    hidden = activated.astype(jnp.bfloat16)
    output = (
        residual
        + jnp.einsum("rsf,fd->rsd", hidden, down_weight, preferred_element_type=jnp.float32)
        + down_bias
    ).astype(jnp.bfloat16)
    cot_values = cotangent.astype(jnp.float32)
    grad_down_weight = jnp.einsum(
        "rsf,rsd->fd", hidden, cotangent, preferred_element_type=jnp.float32
    )
    grad_down_bias = jnp.sum(cot_values, axis=(0, 1))
    grad_hidden = jnp.einsum(
        "rsd,fd->rsf", cotangent, down_weight, preferred_element_type=jnp.float32
    )
    grad_pre = gelu_pullback(grad_hidden)[0].astype(jnp.bfloat16)
    grad_up_weight = jnp.einsum(
        "rsd,rsf->df", normed_two, grad_pre, preferred_element_type=jnp.float32
    )
    grad_up_bias = jnp.sum(grad_pre.astype(jnp.float32), axis=(0, 1))
    grad_normed_two = jnp.einsum(
        "rsf,df->rsd", grad_pre, up_weight, preferred_element_type=jnp.float32
    )
    grad_residual_part, grad_second_gain, grad_second_shift = second_pullback(grad_normed_two)
    grad_residual = cot_values + grad_residual_part
    grad_branch = grad_residual.astype(jnp.bfloat16)
    grad_output_weight = jnp.einsum(
        "rsd,rse->de", mixed_low, grad_branch, preferred_element_type=jnp.float32
    )
    grad_output_bias = jnp.sum(grad_branch.astype(jnp.float32), axis=(0, 1))
    grad_mixed = jnp.einsum(
        "rse,de->rsd", grad_branch, output_weight, preferred_element_type=jnp.float32
    )
    grad_conv = grad_mixed * gate_zero
    grad_gate_zero = grad_mixed * conv_full
    grad_filter_bias = jnp.sum(grad_conv * gated, axis=(0, 1))
    grad_conv_columns = lax.all_to_all(
        grad_conv.astype(jnp.bfloat16), "seq", split_axis=2, concat_axis=1, tiled=True
    ).astype(grad_conv.dtype)
    grad_real, grad_imag = forward_spectrum(grad_conv_columns, tables)
    back_real = filter_real * grad_real + filter_imag * grad_imag
    back_imag = filter_real * grad_imag - filter_imag * grad_real
    grad_gated_columns = inverse_half(back_real, back_imag, tables)
    taps_real = jnp.sum(gated_real * grad_real + gated_imag * grad_imag, axis=0, keepdims=True)
    taps_imag = jnp.sum(gated_real * grad_imag - gated_imag * grad_real, axis=0, keepdims=True)
    grad_filter_columns = inverse_half(taps_real, taps_imag, tables)
    grad_gated_rows, grad_filter_rows = (
        lax.all_to_all(
            shortened(grad_gated_columns), "seq", split_axis=1, concat_axis=2, tiled=True
        ).astype(grad_gated_columns.dtype),
        lax.all_to_all(
            shortened(grad_filter_columns), "seq", split_axis=1, concat_axis=2, tiled=True
        ).astype(grad_filter_columns.dtype),
    )
    filter_grads = filter_pullback(grad_filter_rows[0])
    grad_filter_weight = filter_grads[4]
    grad_decay_rates = filter_grads[5]
    grad_gated = grad_gated_rows + filter_bias * grad_conv
    grad_short = jnp.concatenate(
        [grad_gate_zero, grad_gated * value_part, grad_gated * gate_one], axis=-1
    )
    grad_short_bias = jnp.sum(grad_short, axis=(0, 1))
    grad_short_kernel = jnp.stack(
        [
            jnp.sum(grad_short * proj_values, axis=(0, 1)),
            jnp.sum(grad_short * keep_one_col * lag_one, axis=(0, 1)),
            jnp.sum(grad_short * keep_two_col * lag_two, axis=(0, 1)),
        ]
    )
    tap_one = short_kernel[1] * keep_one_col * grad_short
    tap_two = short_kernel[2] * keep_two_col * grad_short
    outgoing = jnp.concatenate([tap_two[:, 0:1], tap_one[:, 0:1] + tap_two[:, 1:2]], axis=1)
    incoming = from_behind(shortened(outgoing), "seq", -1).astype(outgoing.dtype)
    grad_proj = (
        short_kernel[0] * grad_short
        + jnp.concatenate(
            [tap_one[:, 1:], jnp.zeros((row_count, 1, stream_width), jnp.float32)], axis=1
        )
        + jnp.concatenate(
            [tap_two[:, 2:], jnp.zeros((row_count, 2, stream_width), jnp.float32)], axis=1
        )
    )
    rim_terms = jnp.concatenate(
        [
            jnp.zeros((row_count, local_count - 2, stream_width), jnp.float32),
            incoming[:, 0:1] * keep_one_col[:, -1:],
            incoming[:, 1:2],
        ],
        axis=1,
    )
    grad_proj_low = (grad_proj + rim_terms).astype(jnp.bfloat16)
    grad_input_weight = jnp.einsum(
        "rsd,rse->de", normed, grad_proj_low, preferred_element_type=jnp.float32
    )
    grad_input_bias = jnp.sum(grad_proj_low.astype(jnp.float32), axis=(0, 1))
    grad_normed = jnp.einsum(
        "rse,de->rsd", grad_proj_low, input_weight, preferred_element_type=jnp.float32
    )
    grad_token_part, grad_first_gain, grad_first_shift = first_pullback(grad_normed)
    grad_tokens = (grad_residual + grad_token_part).astype(jnp.bfloat16)
    summed = lax.psum(
        (
            grad_first_gain,
            grad_first_shift,
            grad_input_weight,
            grad_input_bias,
            grad_short_kernel,
            grad_short_bias,
            filter_grads[0],
            filter_grads[1],
            filter_grads[2],
            filter_grads[3],
            grad_filter_weight,
            grad_decay_rates,
            grad_filter_bias,
            grad_output_weight,
            grad_output_bias,
            grad_second_gain,
            grad_second_shift,
            grad_up_weight,
            grad_up_bias,
            grad_down_weight,
            grad_down_bias,
        ),
        "seq",
    )
    summed = tuple(summed)
    return (output, grad_tokens) + summed


def solution(mesh):
    return jax.shard_map(
        shards,
        mesh=mesh,
        in_specs=(
            P(None, "seq", None),
            P(),
            P(),
            P(),
            P(),
            P(),
            P(),
            P(),
            P(),
            P(),
            P(),
            P(),
            P(),
            P(),
            P(),
            P(),
            P(),
            P(),
            P(),
            P(),
            P(),
            P(),
            P(),
            P(None, "seq", None),
        ),
        out_specs=(
            P(None, "seq", None),
            P(None, "seq", None),
            P(),
            P(),
            P(),
            P(),
            P(),
            P(),
            P(),
            P(),
            P(),
            P(),
            P(),
            P(),
            P(),
            P(),
            P(),
            P(),
            P(),
            P(),
            P(),
            P(),
            P(),
        ),
        check_vma=False,
    )
```

profile of v0, /device:TPU:0, one launch (start us, length us, event | category | flops | bytes accessed | tf_op | source)
XLA Modules:
  0.0 992.3 jit_solution(14004255950969521183)
XLA Ops:
  22.4 7.4 all-to-all-start.1
  50.0 8.4 all-to-all-start
  76.8 3.7 reshape.327
  102.0 5.5 copy.287
  107.5 6.6 reshape.376
  114.1 5.7 all-to-all-start.2
  121.6 11.3 %all-to-all-done.2 = bf16[32,2,3072]{2,1,0:T(2,128)(2,1)} async-done(((bf16[32,2,3072]{2,1,0:T(2,128)(2,1)}), bf16[32,2,3072]{2,1,0:T(2,128)(2,1)}, u32[]{:S(2)}, u32[]{:S(2)}) %all-to-all-start.2) | async-done | bytes 393248 | tf_op jit(solution)/shard_map/all_to_all | solution.py:225
  132.9 7.7 reshape.377
  140.6 3.9 copy.234
  147.6 3.5 copy.235
  156.9 4.0 fusion.8
  160.9 7.0 convert_reduce_fusion
  170.1 5.3 convolution_bitcast_fusion.1
  187.6 3.5 all-to-all-start.3
  194.2 7.0 convolution_bitcast_fusion
  237.2 4.1 reshape.366
  241.3 13.4 %reduce.11 = bf16[2048,24]{1,0:T(8,128)(2,1)} reduce(bf16[2048,1,24]{2,1,0:T(2,128)(2,1)} %bitcast.425, bf16[]{:T(256)} %broadcast.460), dimensions={1}, to_apply=%bitcast.363.reduce_sub_computation | reduce | bytes 196610
  260.6 4.4 convolution_add_fusion.1
  270.7 5.5 copy.292
  276.2 6.6 reshape.380
  282.8 6.1 all-to-all-start.4
  288.9 3.8 reshape.383
  312.1 7.7 reshape.381
  319.8 3.9 copy.248
  326.5 3.5 copy.249
  347.6 5.6 convolution_bitcast_fusion.2
  354.0 6.1 fusion.93
  360.1 143.5 %all-reduce.8.cloned.1.call-done = (f32[768]{0:T(1024)}, f32[768]{0:T(1024)}, f32[2304]{0:T(1024)}, f32[3,2304]{1,0:T(4,128)}, f32[2304]{0:T(1024)}, /*index=5*/...) async-done(((f32[768]{0:T(1024)}, f32[768]{0:T(1024)}, ...) | async-done | bytes 108304 | tf_op jit(solution)/shard_map/psum | solution.py:341
  503.6 449.5 %all-reduce.10.cloned.1.call-done = (f32[768,2304]{1,0:T(8,128)}, f32[64,768]{1,0:T(8,128)}, f32[768,768]{1,0:T(8,128)}, f32[768,3072]{1,0:T(8,128)}, f32[3072,768]{1,0:T(8,128)}) async-done(((f32[768,2304]{1,0:T(8,128)}, f32[64,768]{1,0:T(8,128)}, f32[768,768]{1,0:T(8,128)}, f32[768,3072]{1,0:T(8,128)}, f32[3072,768]{1,0:T(8,128)}), (f32[768,2304]{1,0:T(8,128)}, f32[64,768]{1,0:T(8,128)}, ...) | async-done | bytes 28508176 | tf_op jit(solution)/shard_map/psum | solution.py:341
  955.7 6.6 copy.321
  971.5 8.8 copy.336
  980.8 3.7 copy.338
  (389 shorter events, 203.4 us)
Async XLA Ops:
  7.2 28.7 %copy-start = (bf16[768,2304]{1,0:T(8,128)(2,1)S(1)}, bf16[768,2304]{1,0:T(8,128)(2,1)}, u32[]{:S(2)}) copy-start(bf16[768,2304]{1,0:T(8,128)(2,1)} %param.28) | copy-start | bytes 10616836
  11.6 21.1 %copy-start.98 = (s32[4,16]{1,0:T(4,128)S(1)}, s32[4,16]{1,0:T(4,128)}, u32[]{:S(2)}) copy-start(s32[4,16]{1,0:T(4,128)} %param.25) | copy-start | bytes 772
  22.4 27.6 %all-to-all-start.1 = ((bf16[32,2,768]{2,1,0:T(2,128)(2,1)}), bf16[32,2,768]{2,1,0:T(2,128)(2,1)}, u32[]{:S(2)}, u32[]{:S(2)}) async-start(bf16[32,2,768]{2,1,0:T(2,128)(2,1)} %reshape.374), calls=%async_computation.1 | async-start | bytes 196608 | tf_op jit(solution)/shard_map/all_to_all | solution.py:215
  38.3 3.0 collective-permute-start
  50.0 21.6 %all-to-all-start = ((bf16[32,2,3072]{2,1,0:T(2,128)(2,1)}), bf16[32,2,3072]{2,1,0:T(2,128)(2,1)}, u32[]{:S(2)}, u32[]{:S(2)}) async-start(bf16[32,2,3072]{2,1,0:T(2,128)(2,1)} %reshape.372), calls=%async_computation | async-start | bytes 786432 | tf_op jit(solution)/shard_map/all_to_all | solution.py:212
  114.1 18.8 %all-to-all-start.2 = ((bf16[32,2,3072]{2,1,0:T(2,128)(2,1)}), bf16[32,2,3072]{2,1,0:T(2,128)(2,1)}, u32[]{:S(2)}, u32[]{:S(2)}) async-start(bf16[32,2,3072]{2,1,0:T(2,128)(2,1)} %reshape.376), calls=%async_computation.2 | async-start | bytes 786432 | tf_op jit(solution)/shard_map/all_to_all | solution.py:225
  156.6 18.9 %copy-start.20 = (f32[4,64,768]{2,1,0:T(8,128)}, f32[4,64,768]{2,1,0:T(8,128)S(1)}, u32[]{:S(2)}) copy-start(f32[4,64,768]{2,1,0:T(8,128)S(1)} %get-tuple-element.86) | copy-start | bytes 2359300
  156.9 11.0 %slice-start.3 = ((s8[4718592]{0:T(1024)(128)(4,1)}), s8[4194304]{0:T(1024)(128)(4,1)S(1)}, s32[]{:S(2)}) async-start(s8[4718592]{0:T(1024)(128)(4,1)} %bitcast.423), calls=%async_computation.11 | async-start | bytes 8388608
  160.9 7.0 copy-start.35
  187.6 16.7 %all-to-all-start.3 = ((bf16[32,2,3072]{2,1,0:T(2,128)(2,1)}), bf16[32,2,3072]{2,1,0:T(2,128)(2,1)}, u32[]{:S(2)}, u32[]{:S(2)}) async-start(bf16[32,2,3072]{2,1,0:T(2,128)(2,1)} %reshape.378), calls=%async_computation.3 | async-start | bytes 786432 | tf_op jit(solution)/shard_map/all_to_all | solution.py:277
  257.1 25.7 %all-to-all-start.5 = ((bf16[32,2,768]{2,1,0:T(2,128)(2,1)}), bf16[32,2,768]{2,1,0:T(2,128)(2,1)}, u32[]{:S(2)}, u32[]{:S(2)}) async-start(bf16[32,2,768]{2,1,0:T(2,128)(2,1)} %reshape.382), calls=%async_computation.5 | async-start | bytes 196608 | tf_op jit(solution)/shard_map/all_to_all | solution.py:291
  282.8 29.3 %all-to-all-start.4 = ((bf16[32,2,3072]{2,1,0:T(2,128)(2,1)}), bf16[32,2,3072]{2,1,0:T(2,128)(2,1)}, u32[]{:S(2)}, u32[]{:S(2)}) async-start(bf16[32,2,3072]{2,1,0:T(2,128)(2,1)} %reshape.380), calls=%async_computation.4 | async-start | bytes 786432 | tf_op jit(solution)/shard_map/all_to_all | solution.py:288
  288.8 214.8 %all-reduce.8.cloned.1.call-start = ((), (), s32[]{:S(2)}) async-start(), calls=%async_computation.6 | async-start | bytes 321536 | tf_op jit(solution)/shard_map/psum | solution.py:341
  292.7 9.0 copy-start.56
  292.7 9.0 copy-start.85
  296.0 10.9 %copy-start.58 = (f32[64,16]{0,1:T(8,128)S(1)}, f32[64,16]{0,1:T(8,128)}, u32[]{:S(2)}) copy-start(f32[64,16]{0,1:T(8,128)} %copy-done.57) | copy-start | bytes 12292
  338.0 3.1 collective-permute-start.1
  347.3 605.8 %all-reduce.10.cloned.1.call-start = ((), (), s32[]{:S(2)}) async-start(), calls=%async_computation.7 | async-start | bytes 57016320 | tf_op jit(solution)/shard_map/psum | solution.py:341
  955.6 7.3 copy-start.60
  955.6 7.9 copy-start.82
  955.6 8.5 copy-start.69
  955.6 9.1 copy-start.103
  955.6 9.6 copy-start.67
  955.6 10.2 %copy-start.102 = (f32[64]{0:T(128)S(1)}, f32[64]{0:T(128)}, u32[]{:S(2)}) copy-start(f32[64]{0:T(128)} %get-tuple-element.109) | copy-start | bytes 772
  955.7 10.7 %copy-start.47 = (f32[64,768]{1,0:T(8,128)S(1)}, f32[64,768]{1,0:T(8,128)}, u32[]{:S(2)}) copy-start(f32[64,768]{1,0:T(8,128)} %get-tuple-element.110) | copy-start | bytes 589828
  955.7 11.4 %copy-start.94 = (f32[768]{0:T(1024)S(1)}, f32[768]{0:T(1024)}, u32[]{:S(2)}) copy-start(f32[768]{0:T(1024)} %get-tuple-element.111) | copy-start | bytes 9220
  955.7 12.0 %copy-start.93 = (f32[768]{0:T(1024)S(1)}, f32[768]{0:T(1024)}, u32[]{:S(2)}) copy-start(f32[768]{0:T(1024)} %get-tuple-element.112) | copy-start | bytes 9220
  955.7 12.5 %copy-start.37 = (f32[768,768]{1,0:T(8,128)S(1)}, f32[768,768]{1,0:T(8,128)}, u32[]{:S(2)}) copy-start(f32[768,768]{1,0:T(8,128)} %get-tuple-element.113) | copy-start | bytes 7077892
  968.2 12.6 %slice-start = ((s8[9437184]{0:T(1024)(128)(4,1)}), s8[4194304]{0:T(1024)(128)(4,1)S(1)}, s32[]{:S(2)}) async-start(s8[9437184]{0:T(1024)(128)(4,1)} %bitcast.413), calls=%async_computation.8 | async-start | bytes 8388608
  971.5 8.8 copy-start.81
  971.5 9.4 slice-start.1
  971.5 9.4 slice-start.2
  (87 other events, 225.9 us)
Sparse Core Ops, SparseCore 0:
  347.4 156.1 all-reduce.7
  513.2 439.8 all-reduce.9
where the time goes:
time: 1000 us; the launch traced here: 992 us
  waiting for transfers between devices  608 us (61%)
  local copies, waits for them, and re-layouts  167 us (17%)
  matrix products  121 us (12%)
  other arithmetic  42.1 us (4%)
  starting transfers between devices  38.2 us (4%)
  between operations  15.9 us (2%)
    psum x2, waiting for transfers between devices, shards(): lax.psum((grad_first_gain, grad_first_shift, grad_input_weight, grad_inpu...  593 us
    unnamed x253, local copies, waits for them, and re-layouts  90.4 us
    dot_general x12, matrix products, second_back(): jnp.einsum('...kjc,bj->...kbc', values, matrix, precision=HIGHEST_PRECISION)  20.7 us
  transfers between devices with their start and end apart: 10, of which 6 were waited for; matrix products, arithmetic and copies ran while one was open for 10% of the time, Pallas kernels for 0%

commit v1 on v0

v1 whole, which is shorter than its diff:
```python
import functools
import math

import jax
import jax.numpy as jnp
from jax import lax
from jax.experimental import pallas as pl
from jax.experimental.pallas import tpu as pltpu
from jax.sharding import PartitionSpec as P

MESH = pl.DeviceIdType.MESH
EPSILON = 1e-05


def bit_of(me, bit):
    return lax.rem(lax.div(me, bit), 2)

def partner_of(me, bit):
    return me + bit - 2 * bit * bit_of(me, bit)

def halving_plan(rows, columns, order, row_unit, column_unit=128):
    steps = []
    for bit in order:
        if rows % (2 * row_unit) == 0:
            rows //= 2
            steps.append((bit, "row", rows, columns))
        elif columns % (2 * column_unit) == 0:
            columns //= 2
            steps.append((bit, "column", rows, columns))
        else:
            steps.append((bit, "full", rows, columns))
    return steps

class Reduction:
    def __init__(self, array, plan, inbox, sends, arrivals, free, me):
        self.array, self.plan, self.inbox = array, plan, inbox
        self.sends, self.arrivals, self.free, self.me = sends, arrivals, free, me
        self.row, self.column = 0, 0
        self.origin = []
        for bit, kind, rows, columns in plan:
            mine = bit_of(me, bit)
            keep, give = (self.row, self.column), (self.row, self.column)
            if kind == "row":
                keep = (self.row + mine * rows, self.column)
                give = (self.row + (1 - mine) * rows, self.column)
            elif kind == "column":
                keep = (self.row, self.column + mine * columns)
                give = (self.row, self.column + (1 - mine) * columns)
            self.origin.append((keep, give))
            self.row, self.column = keep
        self.unit_rows = plan[-1][2]
        self.unit_columns = plan[-1][3]
        self.unit_columns = min(p[3] for p in plan)
        self.unit_rows = min(p[2] for p in plan)

    def window(self, ref, origin, rows, columns):
        row, column = origin
        if not isinstance(row, int):
            row = pl.multiple_of(row, self.unit_rows)
        if not isinstance(column, int):
            column = pl.multiple_of(column, self.unit_columns)
        return ref.at[pl.ds(row, rows), pl.ds(column, columns)]

    def give_copy(self, s):
        bit, kind, rows, columns = self.plan[s]
        return pltpu.make_async_remote_copy(
            src_ref=self.window(self.array, self.origin[s][1], rows, columns),
            dst_ref=self.inbox[s],
            send_sem=self.sends.at[s], recv_sem=self.arrivals.at[s],
            device_id=(partner_of(self.me, bit),), device_id_type=MESH)

    def share_copy(self, s):
        bit, kind, rows, columns = self.plan[s]
        here = self.window(self.array, self.origin[s][0], rows, columns)
        n = len(self.plan)
        return pltpu.make_async_remote_copy(
            src_ref=here, dst_ref=here,
            send_sem=self.sends.at[n + s], recv_sem=self.arrivals.at[n + s],
            device_id=(partner_of(self.me, bit),), device_id_type=MESH)

    def give(self, s):
        self.give_copy(s).start()

    def take(self, s):
        self.give_copy(s).wait()
        bit, kind, rows, columns = self.plan[s]
        if kind != "full":
            pl.semaphore_signal(
                self.free.at[s], inc=1, device_id=(partner_of(self.me, bit),), device_id_type=MESH
            )
        row, column = self.origin[s][0]
        if not isinstance(column, int):
            column = pl.multiple_of(column, self.unit_columns)
        chunk = self.unit_rows
        inbox = self.inbox[s]
        array = self.array
        def body(i, carry):
            at = pl.multiple_of(i * chunk, chunk)
            here = (pl.ds(pl.multiple_of(row + at, chunk), chunk), pl.ds(column, columns))
            total = array[here].astype(jnp.float32) + inbox[pl.ds(at, chunk), :].astype(jnp.float32)
            array[here] = total.astype(array.dtype)
            return carry
        lax.fori_loop(0, rows // chunk, body, 0)

    def share(self, s):
        if self.plan[s][1] != "full":
            pl.semaphore_wait(self.free.at[s], 1)
            self.share_copy(s).start()

    def collect(self, s):
        if self.plan[s][1] != "full":
            self.share_copy(s).wait()

def inbox_shapes(plan, dtype):
    return [pltpu.VMEM((rows, columns), dtype) for _, _, rows, columns in plan]

def greet_partners(me, n):
    barrier = pltpu.get_barrier_semaphore()
    bit = 1
    count = 0
    while bit < n:
        pl.semaphore_signal(barrier, inc=1, device_id=(partner_of(me, bit),), device_id_type=MESH)
        bit *= 2
        count += 1
    pl.semaphore_wait(barrier, count)

def reduce_kernel(plans, *refs):
    k = len(plans)
    ins, outs, refs = refs[:k], refs[k:2 * k], refs[2 * k:]
    arrays, refs = refs[:k], refs[k:]
    inboxes = []
    for plan in plans:
        inboxes.append(refs[:len(plan)])
        refs = refs[len(plan):]
    sends, refs = refs[:k], refs[k:]
    arrivals, refs = refs[:k], refs[k:]
    free, refs = refs[:k], refs[k:]
    load_sem, store_sem = refs
    me = lax.axis_index("seq")
    n = lax.axis_size("seq")
    loads = [pltpu.make_async_copy(a, b, load_sem.at[i]) for i, (a, b) in enumerate(zip(ins, arrays))]
    for c in loads: c.start()
    greet_partners(me, n)
    work = [Reduction(arrays[i], plans[i], inboxes[i], sends[i], arrivals[i], free[i], me) for i in range(k)]
    steps = len(plans[0])
    for c, w in zip(loads, work):
        c.wait()
        w.give(0)
    for s in range(steps):
        for w in work:
            w.take(s)
            if s + 1 < steps: w.give(s + 1)
            else: w.share(s)
    for s in reversed(range(steps)):
        for w in work:
            w.collect(s)
            if s > 0: w.share(s - 1)
    stores = [pltpu.make_async_copy(b, a, store_sem.at[i]) for i, (a, b) in enumerate(zip(outs, arrays))]
    for c in stores: c.start()
    for c in stores: c.wait()

def default_orders(n):
    bits = []
    b = 1
    while b < n:
        bits.append(b); b *= 2
    core, rest = bits[:1], bits[1:]
    x, y, z = rest[0:1], rest[1:2], rest[2:]
    return [core + x + y + z, core + y + x + z, core + z + x + y]

def all_reduce(arrays, orders, collective_id):
    plans = []
    for a, order in zip(arrays, orders):
        unit = 8 if a.dtype == jnp.float32 else 16
        plans.append(halving_plan(a.shape[0], a.shape[1], order, unit))
    k = len(arrays)
    scratch = [pltpu.VMEM(a.shape, a.dtype) for a in arrays]
    for a, plan in zip(arrays, plans):
        scratch += inbox_shapes(plan, a.dtype)
    for plan in plans + plans:
        scratch.append(pltpu.SemaphoreType.DMA((2 * len(plan),)))
    for plan in plans:
        scratch.append(pltpu.SemaphoreType.REGULAR((len(plan),)))
    scratch += [pltpu.SemaphoreType.DMA((k,)), pltpu.SemaphoreType.DMA((k,))]
    return pl.pallas_call(
        functools.partial(reduce_kernel, plans),
        out_shape=[jax.ShapeDtypeStruct(a.shape, a.dtype) for a in arrays],
        in_specs=[pl.BlockSpec(memory_space=pl.ANY)] * k,
        out_specs=[pl.BlockSpec(memory_space=pl.ANY)] * k,
        scratch_shapes=scratch,
        compiler_params=pltpu.CompilerParams(collective_id=collective_id, has_side_effects=True, vmem_limit_bytes=62 << 20),
        name="reduce_gradients",
    )(*arrays)


HIGHEST = lax.Precision.HIGHEST
LANES = 128

def ceil8(v):
    return -(-v // 8) * 8

def sin_cos(x):
    turns = jnp.round(x * (2.0 / math.pi))
    r = ((x - turns * 1.5703125) - turns * 4.837512969970703125e-4) - turns * 7.54978995489188e-8
    quadrant = turns.astype(jnp.int32)
    z = r * r
    s = ((-1.9515295891e-4 * z + 8.3321608736e-3) * z - 1.6666654611e-1) * z * r + r
    c = ((2.443315711809948e-5 * z - 1.388731625493765e-3) * z + 4.166664568298827e-2) * z * z - 0.5 * z + 1.0
    swap = (quadrant & 1) == 1
    sin_part = jnp.where(swap, c, s)
    cos_part = jnp.where(swap, s, c)
    sin_out = jnp.where((quadrant & 2) == 2, -sin_part, sin_part)
    cos_out = jnp.where(((quadrant + 1) & 2) == 2, -cos_part, cos_part)
    return sin_out, cos_out

def dot(a, b, ca, cb, precision=None):
    return lax.dot_general(a, b, (((ca,), (cb,)), ((), ())), precision=precision, preferred_element_type=jnp.float32)

class Sizes:
    def __init__(self, n, rows, local, width, emb, filt):
        self.n, self.rows, self.local, self.width, self.emb, self.filt = n, rows, local, width, emb, filt
        self.length = n * local
        self.cpd = width // n
        self.cpad = ceil8(self.cpd)
        self.nb = self.length // LANES
        self.tokens = rows * local
        self.tiles = self.tokens // LANES
        self.erows = ceil8(emb)
        assert local * 2 == LANES and rows == 4

def own_selection(z, me):
    want = lax.broadcasted_iota(jnp.int32, (z.cpad, z.width), 0)
    have = lax.broadcasted_iota(jnp.int32, (z.cpad, z.width), 1)
    return jnp.where((have == want + me * z.cpd) & (want < z.cpd), 1.0, 0.0).astype(jnp.float32)

def embed_rows(z, at, count):
    row = lax.broadcasted_iota(jnp.int32, (z.erows, count), 0)
    t = at + lax.broadcasted_iota(jnp.int32, (z.erows, count), 1)
    bands = (z.emb - 1) // 2
    harmonic = jnp.where(row <= bands, row, row - bands)
    angle = lax.rem(t * harmonic, z.length).astype(jnp.float32) * (2.0 * math.pi / z.length)
    s, c = sin_cos(angle)
    scaled = t.astype(jnp.float32) / z.length
    return jnp.where(row == 0, scaled, jnp.where(row <= bands, c, jnp.where(row < z.emb, s, 0.0)))

def columns(ref, count):
    eye = (lax.broadcasted_iota(jnp.int32, (count, count), 0) == lax.broadcasted_iota(jnp.int32, (count, count), 1)).astype(jnp.float32)
    return dot(eye, jnp.broadcast_to(ref[...], (8, count)), 1, 1, HIGHEST)[:, 0:1]

CHUNK = 512

def filter_forward(z, me, w, keep):
    select = own_selection(z, me)
    own_filter = dot(select, w["filter_weight"][...], 1, 1, HIGHEST)
    own_decay = dot(select, jnp.broadcast_to(w["decay_rates"][...], (8, z.width)), 1, 1, HIGHEST)[:, 0:1]
    keep["own_filter"][...] = own_filter
    keep["own_decay"][...] = jnp.broadcast_to(own_decay, (z.cpad, LANES))
    keep["embed_pad"][...] = jnp.zeros((z.erows, z.filt), jnp.float32)
    keep["embed_pad"][0:z.emb, :] = w["embed_weight"][...]
    bias_one = columns(w["embed_bias"], z.filt)
    bias_two = columns(w["inner_bias"], z.filt)
    def body(i, carry):
        at = pl.multiple_of(i * CHUNK, CHUNK)
        here = (slice(None), pl.ds(at, CHUNK))
        embedded = embed_rows(z, at, CHUNK)
        s1, c1 = sin_cos(dot(keep["embed_pad"][...], embedded, 0, 0, HIGHEST) + bias_one)
        s2, c2 = sin_cos(dot(w["inner_weight"][...], s1, 0, 0, HIGHEST) + bias_two)
        raw = dot(own_filter, s2, 1, 0, HIGHEST)
        scaled = (at + lax.broadcasted_iota(jnp.int32, (z.cpad, CHUNK), 1)).astype(jnp.float32) / z.length
        keep["s1"][here] = s1
        keep["c1"][here] = c1
        keep["s2"][here] = s2
        keep["c2"][here] = c2
        keep["taps"][here] = raw * jnp.exp(-own_decay * scaled)
        return carry
    lax.fori_loop(0, z.length // CHUNK, body, 0)

def filter_backward(z, me, w, keep, grad_taps, sums):
    own_filter = keep["own_filter"][...]
    own_decay = keep["own_decay"][:, 0:1]
    for name in ("decay", "filter", "inner", "inner_bias", "embed", "embed_bias"):
        sums[name][...] = jnp.zeros(sums[name].shape, jnp.float32)
    def body(i, carry):
        at = pl.multiple_of(i * CHUNK, CHUNK)
        here = (slice(None), pl.ds(at, CHUNK))
        scaled = (at + lax.broadcasted_iota(jnp.int32, (z.cpad, CHUNK), 1)).astype(jnp.float32) / z.length
        grad = grad_taps[here]
        sums["decay"][...] += jnp.broadcast_to(-jnp.sum(grad * keep["taps"][here] * scaled, axis=1, keepdims=True), (z.cpad, LANES))
        grad_raw = grad * jnp.exp(-own_decay * scaled)
        s2 = keep["s2"][here]
        sums["filter"][...] += dot(grad_raw, s2, 1, 1, HIGHEST)
        two = dot(own_filter, grad_raw, 0, 0, HIGHEST) * keep["c2"][here]
        s1 = keep["s1"][here]
        sums["inner"][...] += dot(s1, two, 1, 1, HIGHEST)
        sums["inner_bias"][...] += jnp.broadcast_to(jnp.sum(two, axis=1, keepdims=True), (z.filt, LANES))
        one = dot(w["inner_weight"][...], two, 1, 0, HIGHEST) * keep["c1"][here]
        sums["embed"][...] += dot(embed_rows(z, at, CHUNK), one, 1, 1, HIGHEST)
        sums["embed_bias"][...] += jnp.broadcast_to(jnp.sum(one, axis=1, keepdims=True), (z.filt, LANES))
        return carry
    lax.fori_loop(0, z.length // CHUNK, body, 0)

def build_toeplitz(z, taps, toeplitz):
    sub = lax.broadcasted_iota(jnp.int32, (8, z.length), 0)
    lane = lax.broadcasted_iota(jnp.int32, (8, LANES), 1)
    sub1 = lax.broadcasted_iota(jnp.int32, (8, LANES), 0)
    def body(c, carry):
        base = jnp.broadcast_to(taps[pl.ds(c, 1), :], (8, z.length))
        for bit in (1, 2, 4):
            base = jnp.where((sub & bit) == bit, pltpu.roll(base, bit, 1), base)
        for q in range(0, LANES // 8, 2):
            parts = []
            for u in (q, q + 1):
                part = pltpu.roll(base, 8 * u, 1) if u else base
                first = jnp.where(lane >= sub1 + 8 * u, part[:, :LANES], 0.0)
                parts.append(jnp.concatenate([first, part[:, LANES:]], axis=1))
            toeplitz[c, 8 * q:8 * q + 16, :] = jnp.concatenate(parts, axis=0).astype(jnp.bfloat16)
        return carry
    lax.fori_loop(0, z.cpd, body, 0)

def fold_toeplitz(z, product):
    lane = lax.broadcasted_iota(jnp.int32, (8, LANES), 1)
    sub1 = lax.broadcasted_iota(jnp.int32, (8, LANES), 0)
    sub = lax.broadcasted_iota(jnp.int32, (8, z.length), 0)
    total = None
    for u in range(LANES // 8):
        part = product[8 * u:8 * u + 8, :]
        first = jnp.where(lane >= sub1 + 8 * u, part[:, :LANES], 0.0)
        part = jnp.concatenate([first, part[:, LANES:]], axis=1)
        part = pltpu.roll(part, z.length - 8 * u, 1) if u else part
        total = part if total is None else total + part
    for bit in (1, 2, 4):
        total = jnp.where((sub & bit) == bit, pltpu.roll(total, z.length - bit, 1), total)
    return jnp.sum(total, axis=0, keepdims=True)

class Exchange:
    def __init__(self, outgoing, incoming, sends, arrivals, me, n):
        self.outgoing, self.incoming, self.sends, self.arrivals, self.me, self.n = outgoing, incoming, sends, arrivals, me, n
    def copy(self, k):
        to = lax.rem(self.me + k, self.n)
        return pltpu.make_async_remote_copy(
            src_ref=self.outgoing.at[to], dst_ref=self.incoming.at[self.me],
            send_sem=self.sends.at[k], recv_sem=self.arrivals.at[k],
            device_id=(to,), device_id_type=MESH)
    def start(self):
        def body(k, carry):
            self.copy(k).start()
            return carry
        lax.fori_loop(1, self.n, body, 0)
        self.incoming[self.me] = self.outgoing[self.me]
    def wait(self):
        def body(k, carry):
            self.copy(k).wait()
            return carry
        lax.fori_loop(1, self.n, body, 0)

def greet_all(me, n):
    barrier = pltpu.get_barrier_semaphore()
    def body(k, carry):
        pl.semaphore_signal(barrier, inc=1, device_id=(lax.rem(me + k, n),), device_id_type=MESH)
        return carry
    lax.fori_loop(1, n, body, 0)
    pl.semaphore_wait(barrier, n - 1)

def each_slab(z, body):
    if z.cpd % 8 == 0:
        lax.fori_loop(0, z.n, body, 0)
    else:
        for k in range(z.n):
            body(k, 0)

def slabs_from_rows(z, flipped, outgoing):
    def body(k, carry):
        at = k * z.cpd
        if z.cpd % 8 == 0:
            at = pl.multiple_of(at, 8)
        slab = flipped[pl.ds(at, z.cpad), :]
        outgoing[k] = jnp.concatenate([slab[:, :LANES], slab[:, LANES:]], axis=0).astype(outgoing.dtype)
        return carry
    each_slab(z, body)

def rows_from_slabs(z, incoming, flipped):
    def body(k, carry):
        at = k * z.cpd
        if z.cpd % 8 == 0:
            at = pl.multiple_of(at, 8)
        slab = incoming[k].astype(jnp.float32)
        flipped[pl.ds(at, z.cpad), :] = jnp.concatenate([slab[:z.cpad], slab[z.cpad:]], axis=1)
        return carry
    each_slab(z, body)

def widen_slabs(z, incoming, wide):
    def body(j, carry):
        wide[pl.ds(pl.multiple_of(j * 2 * z.cpad, 8), 2 * z.cpad), :] = incoming[j].astype(jnp.float32)
        return carry
    lax.fori_loop(0, z.n, body, 0)

def narrow_slabs(z, wide, outgoing):
    def body(j, carry):
        outgoing[j] = wide[pl.ds(pl.multiple_of(j * 2 * z.cpad, 8), 2 * z.cpad), :].astype(outgoing.dtype)
        return carry
    lax.fori_loop(0, z.n, body, 0)

def channel_blocks(z, wide, c):
    lane = lax.broadcasted_iota(jnp.int32, (z.nb, LANES), 1)
    low = lane < LANES // 2
    out = []
    for t in range(2):
        even = wide[pl.ds(t * z.cpad + c, z.nb, 4 * z.cpad), :]
        odd = wide[pl.ds((2 + t) * z.cpad + c, z.nb, 4 * z.cpad), :]
        out.append(jnp.where(low, even, pltpu.roll(odd, LANES // 2, 1)))
        out.append(jnp.where(low, pltpu.roll(even, LANES // 2, 1), odd))
    return out

def put_channel_blocks(z, wide, c, blocks):
    lane = lax.broadcasted_iota(jnp.int32, (z.nb, LANES), 1)
    low = lane < LANES // 2
    for t in range(2):
        a, b = blocks[2 * t], blocks[2 * t + 1]
        wide[pl.ds(t * z.cpad + c, z.nb, 4 * z.cpad), :] = jnp.where(low, a, pltpu.roll(b, LANES // 2, 1))
        wide[pl.ds((2 + t) * z.cpad + c, z.nb, 4 * z.cpad), :] = jnp.where(low, pltpu.roll(a, LANES // 2, 1), b)

def convolve_forward(z, wide, toeplitz, kept, spread):
    def body(c, carry):
        blocks = channel_blocks(z, wide, c)
        x = jnp.concatenate(blocks, axis=0).astype(jnp.bfloat16)
        kept[c] = x
        spread[...] = jnp.zeros(spread.shape, jnp.float32)
        z_all = dot(x, toeplitz[c], 1, 0)
        for d in range(z.nb):
            for r in range(4):
                spread[r, d:d + z.nb, :] += z_all[r * z.nb:(r + 1) * z.nb, d * LANES:(d + 1) * LANES]
        put_channel_blocks(z, wide, c, [spread[r, 0:z.nb, :] for r in range(4)])
        return carry
    lax.fori_loop(0, z.cpd, body, 0)

def convolve_backward(z, wide, toeplitz, kept, spread, advanced, grad_taps):
    spread[...] = jnp.zeros(spread.shape, jnp.float32)
    def body(c, carry):
        blocks = channel_blocks(z, wide, c)
        for r in range(4):
            spread[r, 0:z.nb, :] = blocks[r]
        for d in range(z.nb):
            advanced[:, d * LANES:(d + 1) * LANES] = jnp.concatenate(
                [spread[r, d:d + z.nb, :] for r in range(4)], axis=0).astype(jnp.bfloat16)
        lagged = advanced[...]
        back = dot(lagged, toeplitz[c], 1, 1)
        put_channel_blocks(z, wide, c, [back[r * z.nb:(r + 1) * z.nb] for r in range(4)])
        product = dot(kept[c].astype(jnp.float32).T.astype(jnp.bfloat16), lagged, 1, 0)
        grad_taps[pl.ds(c, 1), :] = fold_toeplitz(z, product)
        return carry
    lax.fori_loop(0, z.cpd, body, 0)

W_NAMES = ("embed_weight", "embed_bias", "inner_weight", "inner_bias", "filter_weight", "decay_rates")
KEEP_NAMES = ("own_filter", "own_decay", "embed_pad", "s1", "c1", "s2", "c2", "taps")

def keep_shapes(z):
    return {"own_filter": (z.cpad, z.filt), "own_decay": (z.cpad, LANES), "embed_pad": (z.erows, z.filt),
            "s1": (z.filt, z.length), "c1": (z.filt, z.length), "s2": (z.filt, z.length), "c2": (z.filt, z.length),
            "taps": (z.cpad, z.length)}

def forward_kernel(z, gated, *refs):
    w = dict(zip(W_NAMES, refs[:6])); refs = refs[6:]
    conv, toeplitz_out, kept, refs = refs[0], refs[1], refs[2], refs[3:]
    keep = dict(zip(KEEP_NAMES, refs[:8])); refs = refs[8:]
    flipped, outgoing, incoming, outgoing2, incoming2, wide, spread, toeplitz, sends, arrivals, sends2, arrivals2, sem = refs
    me = lax.axis_index("seq")
    flipped[z.width:, :] = jnp.zeros((8, z.tokens), jnp.float32)
    flipped[:z.width, :] = gated[...].T
    slabs_from_rows(z, flipped, outgoing)
    greet_all(me, z.n)
    first = Exchange(outgoing, incoming, sends, arrivals, me, z.n)
    first.start()
    filter_forward(z, me, w, keep)
    build_toeplitz(z, keep["taps"], toeplitz)
    first.wait()
    widen_slabs(z, incoming, wide)
    convolve_forward(z, wide, toeplitz, kept, spread)
    narrow_slabs(z, wide, outgoing2)
    second = Exchange(outgoing2, incoming2, sends2, arrivals2, me, z.n)
    second.start()
    out = pltpu.make_async_copy(toeplitz, toeplitz_out, sem)
    out.start()
    second.wait()
    out.wait()
    rows_from_slabs(z, incoming2, flipped)
    conv[...] = flipped[:z.width, :].T

def forward(z, gated, weights, collective_id):
    V = pl.BlockSpec(memory_space=pltpu.VMEM)
    shapes = keep_shapes(z)
    slab = (z.n, 2 * z.cpad, LANES)
    f32, bf16 = jnp.float32, jnp.bfloat16
    outs = [jax.ShapeDtypeStruct((z.tokens, z.width), f32), jax.ShapeDtypeStruct((z.cpd, LANES, z.length), bf16),
            jax.ShapeDtypeStruct((z.cpd, 4 * z.nb, LANES), bf16)] + [jax.ShapeDtypeStruct(shapes[k], f32) for k in KEEP_NAMES]
    return pl.pallas_call(
        functools.partial(forward_kernel, z), out_shape=outs,
        in_specs=[V] * 7, out_specs=[V, pl.BlockSpec(memory_space=pl.ANY)] + [V] * 9,
        scratch_shapes=[pltpu.VMEM((z.width + 8, z.tokens), f32)] + [pltpu.VMEM(slab, bf16)] * 4
        + [pltpu.VMEM((z.n * 2 * z.cpad, LANES), f32), pltpu.VMEM((4, 2 * z.nb, LANES), f32), pltpu.VMEM((z.cpd, LANES, z.length), bf16)]
        + [pltpu.SemaphoreType.DMA((z.n,))] * 4 + [pltpu.SemaphoreType.DMA],
        compiler_params=pltpu.CompilerParams(collective_id=collective_id, has_side_effects=True, vmem_limit_bytes=60 << 20),
        name="convolution_forward")(gated, *weights)

SUM_NAMES = ("decay", "filter", "inner", "inner_bias", "embed", "embed_bias")
def sum_shapes(z):
    return {"decay": (z.cpad, LANES), "filter": (z.cpad, z.filt), "inner": (z.filt, z.filt), "inner_bias": (z.filt, LANES),
            "embed": (z.erows, z.filt), "embed_bias": (z.filt, LANES)}

def backward_kernel(z, grad_conv, *refs):
    w = dict(zip(W_NAMES, refs[:6])); refs = refs[6:]
    toeplitz_in, kept, refs = refs[0], refs[1], refs[2:]
    keep = dict(zip(KEEP_NAMES, refs[:8])); refs = refs[8:]
    grad_gated, refs = refs[0], refs[1:]
    sums = dict(zip(SUM_NAMES, refs[:6])); refs = refs[6:]
    grad_taps, refs = refs[0], refs[1:]
    flipped, outgoing, incoming, outgoing2, incoming2, wide, spread, toeplitz, advanced, sends, arrivals, sends2, arrivals2, sem = refs
    me = lax.axis_index("seq")
    load = pltpu.make_async_copy(toeplitz_in, toeplitz, sem)
    load.start()
    flipped[z.width:, :] = jnp.zeros((8, z.tokens), jnp.float32)
    flipped[:z.width, :] = grad_conv[...].T
    slabs_from_rows(z, flipped, outgoing)
    greet_all(me, z.n)
    first = Exchange(outgoing, incoming, sends, arrivals, me, z.n)
    first.start()
    load.wait()
    first.wait()
    widen_slabs(z, incoming, wide)
    convolve_backward(z, wide, toeplitz, kept, spread, advanced, grad_taps)
    narrow_slabs(z, wide, outgoing2)
    second = Exchange(outgoing2, incoming2, sends2, arrivals2, me, z.n)
    second.start()
    filter_backward(z, me, w, keep, grad_taps, sums)
    second.wait()
    rows_from_slabs(z, incoming2, flipped)
    grad_gated[...] = flipped[:z.width, :].T

def backward(z, grad_conv, weights, saved, collective_id):
    V = pl.BlockSpec(memory_space=pltpu.VMEM)
    slab = (z.n, 2 * z.cpad, LANES)
    f32, bf16 = jnp.float32, jnp.bfloat16
    shapes = sum_shapes(z)
    outs = [jax.ShapeDtypeStruct((z.tokens, z.width), f32)] + [jax.ShapeDtypeStruct(shapes[k], f32) for k in SUM_NAMES] + [jax.ShapeDtypeStruct((z.cpad, z.length), f32)]
    return pl.pallas_call(
        functools.partial(backward_kernel, z), out_shape=outs,
        in_specs=[V] * 7 + [pl.BlockSpec(memory_space=pl.ANY)] + [V] * 9, out_specs=[V] * 8,
        scratch_shapes=[pltpu.VMEM((z.width + 8, z.tokens), f32)] + [pltpu.VMEM(slab, bf16)] * 4
        + [pltpu.VMEM((z.n * 2 * z.cpad, LANES), f32), pltpu.VMEM((4, 2 * z.nb, LANES), f32), pltpu.VMEM((z.cpd, LANES, z.length), bf16), pltpu.VMEM((4 * z.nb, z.length), bf16)]
        + [pltpu.SemaphoreType.DMA((z.n,))] * 4 + [pltpu.SemaphoreType.DMA],
        compiler_params=pltpu.CompilerParams(collective_id=collective_id, has_side_effects=True, vmem_limit_bytes=60 << 20),
        name="convolution_backward")(grad_conv, *weights, *saved)


def from_behind(block, axis, distance):
    devices = range(lax.axis_size(axis))
    route = [(i - distance, i) for i in devices if i - distance in devices]
    return lax.ppermute(block, axis, route)


def shortened(x):
    return jax.tree.map(lambda a: a.astype(jnp.bfloat16) if a.dtype == jnp.float32 else a, x)


def layer_norm(values, norm_gain, norm_shift):
    center = values - jnp.mean(values, axis=-1, keepdims=True)
    spread = jnp.mean(center * center, axis=-1, keepdims=True)
    return center * lax.rsqrt(spread + EPSILON) * norm_gain + norm_shift


def shards(
    tokens,
    doc_lengths,
    first_gain,
    first_shift,
    input_weight,
    input_bias,
    short_kernel,
    short_bias,
    embed_weight,
    embed_bias,
    inner_weight,
    inner_bias,
    filter_weight,
    decay_rates,
    filter_bias,
    output_weight,
    output_bias,
    second_gain,
    second_shift,
    up_weight,
    up_bias,
    down_weight,
    down_bias,
    cotangent,
):
    row_count, local_count, model_width = tokens.shape
    stream_width = 3 * model_width
    device_count = lax.axis_size("seq")
    seq_length = local_count * device_count
    offset = lax.axis_index("seq") * local_count
    positions = offset + jnp.arange(local_count, dtype=jnp.int32)
    doc_ends = jnp.cumsum(doc_lengths, axis=1)[:, :-1]
    starting = jnp.any(positions[None, :, None] == doc_ends[:, None, :], axis=-1) | (
        positions[None, :] == 0
    )
    keep_one = jnp.where(starting, 0.0, 1.0).astype(jnp.float32)
    keep_two = keep_one * jnp.concatenate(
        [jnp.ones((row_count, 1), jnp.float32), keep_one[:, :-1]], axis=1
    )
    keep_one_col = keep_one[:, :, None]
    keep_two_col = keep_two[:, :, None]
    token_values = tokens.astype(jnp.float32)
    first_norm, first_pullback = jax.vjp(layer_norm, token_values, first_gain, first_shift)
    normed = first_norm.astype(jnp.bfloat16)
    projected = (
        jnp.einsum("rsd,de->rse", normed, input_weight, preferred_element_type=jnp.float32)
        + input_bias
    ).astype(jnp.bfloat16)
    rim_rows = jnp.concatenate(
        [projected[:, -2:-1] * keep_one_col[:, -1:].astype(jnp.bfloat16), projected[:, -1:]], axis=1
    )
    previous = from_behind(rim_rows, "seq", 1)
    extended = jnp.concatenate([previous, projected], axis=1).astype(jnp.float32)
    lag_one = extended[:, 1:-1]
    lag_two = extended[:, :-2]
    proj_values = extended[:, 2:]
    short_out = (
        short_kernel[0] * proj_values
        + short_kernel[1] * keep_one_col * lag_one
        + short_kernel[2] * keep_two_col * lag_two
        + short_bias
    )
    gate_zero = short_out[..., :model_width]
    gate_one = short_out[..., model_width : 2 * model_width]
    value_part = short_out[..., 2 * model_width :]
    gated = value_part * gate_one
    z = Sizes(device_count, row_count, local_count, model_width, embed_weight.shape[0], embed_weight.shape[1])
    filter_weights = (embed_weight, embed_bias[None], inner_weight, inner_bias[None], filter_weight, decay_rates[None])
    conv_rows, *saved = forward(z, gated.reshape(-1, model_width), filter_weights, 0)
    conv_rows = conv_rows.reshape(tokens.shape)
    conv_full = conv_rows + filter_bias * gated
    mixed_low = (conv_full * gate_zero).astype(jnp.bfloat16)
    branch = (
        jnp.einsum("rsd,de->rse", mixed_low, output_weight, preferred_element_type=jnp.float32)
        + output_bias
    )
    residual = token_values + branch
    second_norm, second_pullback = jax.vjp(layer_norm, residual, second_gain, second_shift)
    normed_two = second_norm.astype(jnp.bfloat16)
    pre_active = (
        jnp.einsum("rsd,df->rsf", normed_two, up_weight, preferred_element_type=jnp.float32)
        + up_bias
    )
    activated, gelu_pullback = jax.vjp(functools.partial(jax.nn.gelu, approximate=True), pre_active)
    hidden = activated.astype(jnp.bfloat16)
    output = (
        residual
        + jnp.einsum("rsf,fd->rsd", hidden, down_weight, preferred_element_type=jnp.float32)
        + down_bias
    ).astype(jnp.bfloat16)
    cot_values = cotangent.astype(jnp.float32)
    grad_down_weight = jnp.einsum(
        "rsf,rsd->fd", hidden, cotangent, preferred_element_type=jnp.float32
    )
    grad_down_bias = jnp.sum(cot_values, axis=(0, 1))
    grad_hidden = jnp.einsum(
        "rsd,fd->rsf", cotangent, down_weight, preferred_element_type=jnp.float32
    )
    grad_pre = gelu_pullback(grad_hidden)[0].astype(jnp.bfloat16)
    grad_up_weight = jnp.einsum(
        "rsd,rsf->df", normed_two, grad_pre, preferred_element_type=jnp.float32
    )
    grad_up_bias = jnp.sum(grad_pre.astype(jnp.float32), axis=(0, 1))
    grad_normed_two = jnp.einsum(
        "rsf,df->rsd", grad_pre, up_weight, preferred_element_type=jnp.float32
    )
    grad_residual_part, grad_second_gain, grad_second_shift = second_pullback(grad_normed_two)
    grad_residual = cot_values + grad_residual_part
    grad_branch = grad_residual.astype(jnp.bfloat16)
    grad_output_weight = jnp.einsum(
        "rsd,rse->de", mixed_low, grad_branch, preferred_element_type=jnp.float32
    )
    grad_output_bias = jnp.sum(grad_branch.astype(jnp.float32), axis=(0, 1))
    grad_mixed = jnp.einsum(
        "rse,de->rsd", grad_branch, output_weight, preferred_element_type=jnp.float32
    )
    grad_conv = grad_mixed * gate_zero
    grad_gate_zero = grad_mixed * conv_full
    grad_filter_bias = jnp.sum(grad_conv * gated, axis=(0, 1))
    grad_gated_rows, *sums = backward(z, grad_conv.reshape(-1, model_width), filter_weights, saved, 1)
    grad_gated_rows = grad_gated_rows.reshape(tokens.shape)
    sums = dict(zip(SUM_NAMES, sums))
    device = lax.axis_index("seq")
    owned = jnp.zeros((z.filt + 1, z.width), jnp.float32)
    own_sums = jnp.concatenate([sums["filter"][: z.cpd].T, sums["decay"][: z.cpd, :1].T], axis=0)
    owned = lax.dynamic_update_slice(owned, own_sums, (0, device * z.cpd))
    grad_gated = grad_gated_rows + filter_bias * grad_conv
    grad_short = jnp.concatenate(
        [grad_gate_zero, grad_gated * value_part, grad_gated * gate_one], axis=-1
    )
    grad_short_bias = jnp.sum(grad_short, axis=(0, 1))
    grad_short_kernel = jnp.stack(
        [
            jnp.sum(grad_short * proj_values, axis=(0, 1)),
            jnp.sum(grad_short * keep_one_col * lag_one, axis=(0, 1)),
            jnp.sum(grad_short * keep_two_col * lag_two, axis=(0, 1)),
        ]
    )
    tap_one = short_kernel[1] * keep_one_col * grad_short
    tap_two = short_kernel[2] * keep_two_col * grad_short
    outgoing = jnp.concatenate([tap_two[:, 0:1], tap_one[:, 0:1] + tap_two[:, 1:2]], axis=1)
    incoming = from_behind(shortened(outgoing), "seq", -1).astype(outgoing.dtype)
    grad_proj = (
        short_kernel[0] * grad_short
        + jnp.concatenate(
            [tap_one[:, 1:], jnp.zeros((row_count, 1, stream_width), jnp.float32)], axis=1
        )
        + jnp.concatenate(
            [tap_two[:, 2:], jnp.zeros((row_count, 2, stream_width), jnp.float32)], axis=1
        )
    )
    rim_terms = jnp.concatenate(
        [
            jnp.zeros((row_count, local_count - 2, stream_width), jnp.float32),
            incoming[:, 0:1] * keep_one_col[:, -1:],
            incoming[:, 1:2],
        ],
        axis=1,
    )
    grad_proj_low = (grad_proj + rim_terms).astype(jnp.bfloat16)
    grad_input_weight = jnp.einsum(
        "rsd,rse->de", normed, grad_proj_low, preferred_element_type=jnp.float32
    )
    grad_input_bias = jnp.sum(grad_proj_low.astype(jnp.float32), axis=(0, 1))
    grad_normed = jnp.einsum(
        "rse,de->rsd", grad_proj_low, input_weight, preferred_element_type=jnp.float32
    )
    grad_token_part, grad_first_gain, grad_first_shift = first_pullback(grad_normed)
    grad_tokens = (grad_residual + grad_token_part).astype(jnp.bfloat16)
    small = [
        grad_first_gain,
        grad_first_shift,
        grad_input_bias,
        grad_short_kernel,
        grad_short_bias,
        sums["embed"][: z.emb],
        sums["embed_bias"][:, 0],
        sums["inner"],
        sums["inner_bias"][:, 0],
        owned,
        grad_filter_bias,
        grad_output_bias,
        grad_second_gain,
        grad_second_shift,
        grad_up_bias,
        grad_down_bias,
    ]
    count = sum(v.size for v in small)
    rows = -(-count // (z.width * 128)) * 128
    packed = jnp.concatenate(
        [v.reshape(-1) for v in small] + [jnp.zeros((rows * z.width - count,), jnp.float32)]
    ).reshape(rows, z.width)
    orders = default_orders(device_count)
    large = [grad_down_weight, grad_up_weight, grad_input_weight, grad_output_weight]
    reduced = all_reduce(
        [v.astype(jnp.bfloat16) for v in large] + [packed],
        [orders[0], orders[1], orders[2], orders[0], orders[1]],
        2,
    )
    grad_down_weight, grad_up_weight, grad_input_weight, grad_output_weight = [
        v.astype(jnp.float32) for v in reduced[:4]
    ]
    flat = reduced[4].reshape(-1)
    parts = []
    at = 0
    for v in small:
        parts.append(flat[at : at + v.size].reshape(v.shape))
        at += v.size
    return (
        output,
        grad_tokens,
        parts[0],
        parts[1],
        grad_input_weight,
        parts[2],
        parts[3],
        parts[4],
        parts[5],
        parts[6],
        parts[7],
        parts[8],
        parts[9][: z.filt],
        parts[9][z.filt],
        parts[10],
        grad_output_weight,
        parts[11],
        parts[12],
        parts[13],
        grad_up_weight,
        parts[14],
        grad_down_weight,
        parts[15],
    )


def solution(mesh):
    return jax.shard_map(
        shards,
        mesh=mesh,
        in_specs=(
            P(None, "seq", None),
            P(),
            P(),
            P(),
            P(),
            P(),
            P(),
            P(),
            P(),
            P(),
            P(),
            P(),
            P(),
            P(),
            P(),
            P(),
            P(),
            P(),
            P(),
            P(),
            P(),
            P(),
            P(),
            P(None, "seq", None),
        ),
        out_specs=(
            P(None, "seq", None),
            P(None, "seq", None),
            P(),
            P(),
            P(),
            P(),
            P(),
            P(),
            P(),
            P(),
            P(),
            P(),
            P(),
            P(),
            P(),
            P(),
            P(),
            P(),
            P(),
            P(),
            P(),
            P(),
            P(),
        ),
        check_vma=False,
    )
```

time: 1000 us -> 368 us (0.37)
  waiting for transfers between devices: 608 us -> 0.01 us
  Pallas kernels: 0 us -> 275 us
  local copies, waits for them, and re-layouts: 167 us -> 22.4 us
  matrix products: 121 us -> 31.5 us
  starting transfers between devices: 38.2 us -> 3.65 us
  between operations: 15.9 us -> 1.44 us
    psum x2 -> x0, waiting for transfers between devices: 593 us -> none  [shards(): lax.psum((grad_first_gain, grad_first_shift, grad_input_weight, grad_inpu...]
    pallas_call x0 -> x3, Pallas kernels: none -> 275 us  [the longest x1 179 us: all_reduce(): pl.pallas_call(functools.partial(reduce_kernel, plans), out_shape=[jax.Sh...]
    unnamed x253 -> x84, local copies, waits for them, and re-layouts: 90.4 us -> 1.56 us
    dot_general x44 -> x0, matrix products: 72.8 us -> none  [the longest x12 20.7 us: second_back(): jnp.einsum('...kjc,bj->...kbc', values, matrix, precision=HIGHEST_PRECISION)]
    convert_element_type x16 -> x0, local copies, waits for them, and re-layouts: 47.7 us -> none  [the longest x4 17.7 us: shortened(): a.astype(jnp.bfloat16)]
    all_to_all x6 -> x0, starting transfers between devices: 34.5 us -> none  [the longest x1 8.43 us: shards(): lax.all_to_all(gated.astype(jnp.bfloat16), 'seq', split_axis=2, concat_ax...]
    unnamed x4 -> x3, other arithmetic: 16.8 us -> 0.01 us
    all_to_all x8 -> x0, local copies, waits for them, and re-layouts: 16.4 us -> none  [the longest x1 3.89 us: shards(): lax.all_to_all(shortened(conv_columns), 'seq', split_axis=1, concat_axis=...]
  transfers between devices with their start and end apart: 10 -> 2, of which waited for: 6 -> 0; matrix products, arithmetic and copies ran while one was open for 10% -> 1% of each run, Pallas kernels for 0% -> 0%
where the time goes in v1:
time: 368 us
  Pallas kernels  275 us (75%)
  other arithmetic  33.9 us (9%)
  matrix products  31.5 us (9%)
  local copies, waits for them, and re-layouts  22.4 us (6%)
    pallas_call x1, Pallas kernels, all_reduce(): pl.pallas_call(functools.partial(reduce_kernel, plans), out_shape=[jax.Sh...  179 us
    pallas_call x1, Pallas kernels, backward(): pl.pallas_call(functools.partial(backward_kernel, z), out_shape=outs, in_...  49.1 us
    pallas_call x1, Pallas kernels, forward(): pl.pallas_call(functools.partial(forward_kernel, z), out_shape=outs, in_s...  47.3 us
    convert_element_type x4, other arithmetic, shards(): v.astype(jnp.float32)  17.3 us
    slice x11, local copies, waits for them, and re-layouts, shards(): parts.append(flat[at:at + v.size].reshape(v.shape))  8.73 us
  transfers between devices with their start and end apart: 2, of which 0 were waited for; matrix products, arithmetic and copies ran while one was open for 1% of the time, Pallas kernels for 0%

profile of v1, /device:TPU:0, one launch (start us, length us, event | category | flops | bytes accessed | tf_op | source)
XLA Modules:
  0.0 367.9 jit_solution(17551812425861888158)
XLA Ops:
  0.7 1.2 convert_reduce_fusion.2
  1.9 1.2 fusion.50
  4.5 3.3 fusion.11
  8.0 2.4 collective-permute-start
  14.0 47.3 %convolution_forward.1 = (f32[256,768]{1,0:T(8,128)}, bf16[24,128,2048]{2,1,0:T(8,128)(2,1)}, bf16[24,64,128]{2,1,0:T(8,128)(2,1)}, f32[24,64]{1,0:T(8,128)}, f3...) custom-call(f32[256,768]{1,0:T(8,128)} %bitcast.76, ...), custom_call_target="tpu_custom_call" | custom-call | tf_op jit(solution)/shard_map/convolution_forward/pallas_call | solution.py:495
  61.3 1.3 multiply_convert_fusion.1
  63.6 4.0 %fusion.8 = f32[4,64,3072]{2,1,0:T(8,128)S(1)} fusion(bf16[768,3072]{1,0:T(8,128)(2,1)} %param.43, f32[3072]{0:T(1024)S(1)} %copy-done.28, f32[4,64,768]{2,1,0:T(8,128)S(1)} %get-tuple-element.113, f32[768]{0:T(1024)S(1)} %copy-done.19, f32[768]{0:T(1024)S(1)} %copy-done.18, f32[4,64]{1,0:T(4,128)S(1)} %fusion.60, f32[4,64]{1,0:T(4,128)S(1)} %broadcast_multiply_fusion), kind=kOutput, calls=%fused_computation.14 | convolution fusion | flops 1209729024 | bytes 8671232 | tf_op jit(solution)/shard_map/rsd,df->rsf/dot_general | solution.py:651
  67.6 4.4 %bitcast_convert_fusion.1.refs_0_ = bf16[3072,768]{1,0:T(8,128)(2,1)} fusion(bf16[4,64,768]{2,1,0:T(8,128)(2,1)S(1)} %copy-done.15, f32[4,64,3072]{2,1,0:T(8,128)S(1)} %fusion.8), kind=kOutput, calls=%fused_computation.1 | convolution fusion | flops 1217396736 | bytes 8257536 | tf_op jit(solution)/shard_map/rsf,rsd->fd/dot_general | solution.py:662
  72.1 3.3 convert_reduce_fusion
  75.4 1.7 multiply_reduce_fusion.3
  77.2 3.8 %bitcast_convert_fusion.refs_1_ = bf16[768,3072]{1,0:T(8,128)(2,1)} fusion(bf16[4,64,3072]{2,1,0:T(8,128)(2,1)S(1)} %get-tuple-element.117, f32[4,64,768]{2,1,0:T(8,128)S(1)} %get-tuple-element.113, f32[768]{0:T(1024)S(1)} %copy-done.19, f32[768]{0:T(1024)S(1)} %copy-done.18, f32[4,64]{1,0:T(4,128)S(1)} %fusion.60, f32[4,64]{1,0:T(4,128)S(1)} %broadcast_multiply_fusion), kind=kOutput, calls=%fused_computation | convolution fusion | flops 1211301888 | bytes 7086080 | tf_op jit(solution)/shard_map/rsd,rsf->df/dot_general | solution.py:670
  81.0 2.7 fusion.35
  84.3 1.6 bitcast_convert_fusion.3.refs_3_
  85.9 1.7 multiply_reduce_fusion.4
  87.6 49.1 %convolution_backward.1 = (f32[256,768]{1,0:T(8,128)}, f32[24,128]{1,0:T(8,128)}, f32[24,64]{1,0:T(8,128)}, f32[64,64]{1,0:T(8,128)}, f32[64,128]{1,0:T(8,128)},...) custom-call(f32[256,768]{1,0:T(8,128)} %bitcast.75, f32[33,64]{1,0:T(8,128)} %refs_0_.3, ...), custom_call_target="tpu_custom_call" | custom-call | tf_op jit(solution)/shard_map/convolution_backward/pallas_call | solution.py:544
  136.8 1.7 slice_multiply_fusion.3
  139.2 1.6 multiply_reduce_fusion.2
  141.0 1.3 collective-permute-start.1
  142.5 1.6 slice.213
  144.1 1.6 slice.214
  147.0 3.1 convert_reduce_fusion.1
  150.4 1.2 fusion.63
  151.7 3.1 bitcast_convert_fusion.2.refs_2_
  155.3 1.2 convert_reduce_fusion.3
  156.5 3.3 concatenate.40
  160.6 178.7 %reduce_gradients.1 = (bf16[3072,768]{1,0:T(8,128)(2,1)}, bf16[768,3072]{1,0:T(8,128)(2,1)}, bf16[768,2304]{1,0:T(8,128)(2,1)}, bf16[768,768]{1,0:T(8,128)(2,1)}, f32[128,768]{1,0:T(8,128)}) custom-call(bf16[3072,768]{1,0:T(8,128)(2,1)} %bitcast_convert_fusion.1.refs_0_, bf16[768,3072]{1,0:T(8,128)(2,1)} %bitcast_convert_fusion.refs_1_, ...), custom_call_target="tpu_custom_call" | custom-call | tf_op jit(solution)/shard_map/reduce_gradients/pallas_call | solution.py:185
  339.3 1.5 slice_reduce_fusion.5
  345.5 1.2 slice.191
  350.5 1.6 convert_element_type.102
  352.1 6.2 %convert_element_type.101 = f32[768,2304]{1,0:T(8,128)} convert(bf16[768,2304]{1,0:T(8,128)(2,1)} %get-tuple-element.65) | non-fusion elementwise | flops 1769472 | bytes 10616832 | tf_op jit(solution)/shard_map/convert_element_type | solution.py:771
  358.3 5.0 %convert_element_type.103 = f32[768,3072]{1,0:T(8,128)} convert(bf16[768,3072]{1,0:T(8,128)(2,1)S(1)} %copy-done.13) | non-fusion elementwise | flops 2359296 | bytes 14155776 | tf_op jit(solution)/shard_map/convert_element_type | solution.py:771
  363.4 4.5 %convert_element_type.104 = f32[3072,768]{1,0:T(8,128)} convert(bf16[3072,768]{1,0:T(8,128)(2,1)S(1)} %bitcast.78) | non-fusion elementwise | flops 2359296 | bytes 14155776 | tf_op jit(solution)/shard_map/convert_element_type | solution.py:771
  (156 shorter events, 19.0 us)
Async XLA Ops:
  0.7 62.0 %copy-start = (bf16[768,768]{1,0:T(8,128)(2,1)S(1)}, bf16[768,768]{1,0:T(8,128)(2,1)}, u32[]{:S(2)}) copy-start(bf16[768,768]{1,0:T(8,128)(2,1)} %param.39) | copy-start | bytes 3538948
  4.5 6.0 %copy-start.24 = (f32[3,2304]{1,0:T(4,128)S(1)}, f32[3,2304]{1,0:T(4,128)}, u32[]{:S(2)}) copy-start(f32[3,2304]{1,0:T(4,128)} %param.30) | copy-start | bytes 82948
  4.5 6.2 %copy-start.32 = (f32[768]{0:T(1024)S(1)}, f32[768]{0:T(1024)}, u32[]{:S(2)}) copy-start(f32[768]{0:T(1024)} %param.37) | copy-start | bytes 9220
  7.7 3.8 %copy-start.27 = (f32[2304]{0:T(1024)S(1)}, f32[2304]{0:T(1024)}, u32[]{:S(2)}) copy-start(f32[2304]{0:T(1024)} %param.31) | copy-start | bytes 27652
  8.0 3.3 collective-permute-start
  13.1 48.3 %copy-start.20 = (f32[768]{0:T(1024)S(1)}, f32[768]{0:T(1024)}, u32[]{:S(2)}) copy-start(f32[768]{0:T(1024)} %param.38) | copy-start | bytes 9220
  14.0 48.6 %copy-start.4 = (bf16[4,64,768]{2,1,0:T(8,128)(2,1)S(1)}, bf16[4,64,768]{2,1,0:T(8,128)(2,1)}, u32[]{:S(2)}) copy-start(bf16[4,64,768]{2,1,0:T(8,128)(2,1)} %param.24) | copy-start | bytes 1179652
  14.0 48.7 %copy-start.31 = (f32[768]{0:T(1024)S(1)}, f32[768]{0:T(1024)}, u32[]{:S(2)}) copy-start(f32[768]{0:T(1024)} %param.40) | copy-start | bytes 9220
  63.6 4.0 %copy-start.15 = (bf16[4,64,768]{2,1,0:T(8,128)(2,1)S(1)}, bf16[4,64,768]{2,1,0:T(8,128)(2,1)}, u32[]{:S(2)}) copy-start(bf16[4,64,768]{2,1,0:T(8,128)(2,1)} %param.47) | copy-start | bytes 1179652
  63.6 8.5 %slice-start.4 = ((s8[4718592]{0:T(1024)(128)(4,1)}), s8[4194304]{0:T(1024)(128)(4,1)S(1)}, s32[]{:S(2)}) async-start(s8[4718592]{0:T(1024)(128)(4,1)} %bitcast.91), calls=%async_computation.4 | async-start | bytes 8388608
  63.6 11.8 %slice-start.2 = ((s8[4718592]{0:T(1024)(128)(4,1)}), s8[4194304]{0:T(1024)(128)(4,1)S(1)}, s32[]{:S(2)}) async-start(s8[4718592]{0:T(1024)(128)(4,1)} %bitcast.79), calls=%async_computation.2 | async-start | bytes 8388608
  67.6 4.5 %slice-start.5 = ((s8[4718592]{0:T(1024)(128)(4,1)}), s8[524288]{0:T(1024)(128)(4,1)S(1)}, s32[]{:S(2)}) async-start(s8[4718592]{0:T(1024)(128)(4,1)} %bitcast.91), calls=%async_computation.5 | async-start | bytes 1048576
  67.6 7.8 %slice-start.3 = ((s8[4718592]{0:T(1024)(128)(4,1)}), s8[524288]{0:T(1024)(128)(4,1)S(1)}, s32[]{:S(2)}) async-start(s8[4718592]{0:T(1024)(128)(4,1)} %bitcast.79), calls=%async_computation.3 | async-start | bytes 1048576
  77.2 3.8 %copy-start.34 = (f32[768]{0:T(1024)S(1)}, f32[768]{0:T(1024)}, u32[]{:S(2)}) copy-start(f32[768]{0:T(1024)} %param.46) | copy-start | bytes 9220
  136.8 2.4 copy-start.5
  138.5 2.2 copy-start.6
  138.5 2.2 copy-start.8
  139.2 3.1 copy-start.22
  139.2 3.1 copy-start.23
  139.2 3.3 copy-start.30
  141.0 5.8 %collective-permute-start.1 = (bf16[4,2,2304]{2,1,0:T(2,128)(2,1)S(1)}, bf16[4,2,2304]{2,1,0:T(2,128)(2,1)S(1)}, u32[]{:S(2)}, u32[]{:S(2)}) collective-permute-start(bf16[4,2,2304]{2,1,0:T(2,128)(2,1)S(1)} %pad_maximum_fusion.2), channel_id=1, source_target_pairs={{1,0},{2,1},{3,2},{4,3},{5,4},{6,5},{7,6},{8,7},{9,8},{10,9},{11,1... | collective-permute-start | bytes 110600 | tf_op jit(solution)/shard_map/ppermute | solution.py:557
  144.1 2.8 copy-start.7
  144.1 2.8 copy-start.9
  147.0 3.2 copy-start.26
  147.0 3.4 copy-start.33
  151.6 3.6 copy-start.11
  151.7 3.6 copy-start.16
  339.3 11.3 %copy-start.17 = (bf16[768,768]{1,0:T(8,128)(2,1)S(1)}, bf16[768,768]{1,0:T(8,128)(2,1)}, u32[]{:S(2)}) copy-start(bf16[768,768]{1,0:T(8,128)(2,1)} %get-tuple-element.66) | copy-start | bytes 3538948
  352.1 6.2 %copy-start.13 = (bf16[768,3072]{1,0:T(8,128)(2,1)S(1)}, bf16[768,3072]{1,0:T(8,128)(2,1)}, u32[]{:S(2)}) copy-start(bf16[768,3072]{1,0:T(8,128)(2,1)} %get-tuple-element.67) | copy-start | bytes 14155780
  352.1 11.3 %slice-start = ((s8[4718592]{0:T(1024)(128)(4,1)}), s8[4194304]{0:T(1024)(128)(4,1)S(1)}, s32[]{:S(2)}) async-start(s8[4718592]{0:T(1024)(128)(4,1)} %bitcast.77), calls=%async_computation | async-start | bytes 8388608
  358.3 5.1 %slice-start.1 = ((s8[4718592]{0:T(1024)(128)(4,1)}), s8[524288]{0:T(1024)(128)(4,1)S(1)}, s32[]{:S(2)}) async-start(s8[4718592]{0:T(1024)(128)(4,1)} %bitcast.77), calls=%async_computation.1 | async-start | bytes 1048576
  363.4 4.5 %copy-start.1 = (bf16[768,768]{1,0:T(8,128)(2,1)S(1)}, bf16[768,768]{1,0:T(8,128)(2,1)}, u32[]{:S(2)}) copy-start(bf16[768,768]{1,0:T(8,128)(2,1)} %param.39) | copy-start | bytes 3538948
  (12 other events, 18.0 us)

commit v2 on v1

v2 whole, which is shorter than its diff:
```python
import functools
import math

import jax
import jax.numpy as jnp
from jax import lax
from jax.experimental import pallas as pl
from jax.experimental.pallas import tpu as pltpu
from jax.sharding import PartitionSpec as P

MESH = pl.DeviceIdType.MESH
EPSILON = 1e-05


def bit_of(me, bit):
    return lax.rem(lax.div(me, bit), 2)

def partner_of(me, bit):
    return me + bit - 2 * bit * bit_of(me, bit)

def halving_plan(rows, columns, order, row_unit, column_unit=128):
    steps = []
    for bit in order:
        if rows % (2 * row_unit) == 0:
            rows //= 2
            steps.append((bit, "row", rows, columns))
        elif columns % (2 * column_unit) == 0:
            columns //= 2
            steps.append((bit, "column", rows, columns))
        else:
            steps.append((bit, "full", rows, columns))
    return steps

class Reduction:
    def __init__(self, array, plan, inbox, sends, arrivals, free, me):
        self.array, self.plan, self.inbox = array, plan, inbox
        self.sends, self.arrivals, self.free, self.me = sends, arrivals, free, me
        self.row, self.column = 0, 0
        self.origin = []
        for bit, kind, rows, columns in plan:
            mine = bit_of(me, bit)
            keep, give = (self.row, self.column), (self.row, self.column)
            if kind == "row":
                keep = (self.row + mine * rows, self.column)
                give = (self.row + (1 - mine) * rows, self.column)
            elif kind == "column":
                keep = (self.row, self.column + mine * columns)
                give = (self.row, self.column + (1 - mine) * columns)
            self.origin.append((keep, give))
            self.row, self.column = keep
        self.unit_rows = plan[-1][2]
        self.unit_columns = plan[-1][3]
        self.unit_columns = min(p[3] for p in plan)
        self.unit_rows = min(p[2] for p in plan)

    def window(self, ref, origin, rows, columns):
        row, column = origin
        if not isinstance(row, int):
            row = pl.multiple_of(row, self.unit_rows)
        if not isinstance(column, int):
            column = pl.multiple_of(column, self.unit_columns)
        return ref.at[pl.ds(row, rows), pl.ds(column, columns)]

    def give_copy(self, s):
        bit, kind, rows, columns = self.plan[s]
        return pltpu.make_async_remote_copy(
            src_ref=self.window(self.array, self.origin[s][1], rows, columns),
            dst_ref=self.inbox[s],
            send_sem=self.sends.at[s], recv_sem=self.arrivals.at[s],
            device_id=(partner_of(self.me, bit),), device_id_type=MESH)

    def share_copy(self, s):
        bit, kind, rows, columns = self.plan[s]
        here = self.window(self.array, self.origin[s][0], rows, columns)
        n = len(self.plan)
        return pltpu.make_async_remote_copy(
            src_ref=here, dst_ref=here,
            send_sem=self.sends.at[n + s], recv_sem=self.arrivals.at[n + s],
            device_id=(partner_of(self.me, bit),), device_id_type=MESH)

    def give(self, s):
        self.give_copy(s).start()

    def take(self, s):
        self.give_copy(s).wait()
        bit, kind, rows, columns = self.plan[s]
        if kind != "full":
            pl.semaphore_signal(
                self.free.at[s], inc=1, device_id=(partner_of(self.me, bit),), device_id_type=MESH
            )
        row, column = self.origin[s][0]
        if not isinstance(column, int):
            column = pl.multiple_of(column, self.unit_columns)
        chunk = self.unit_rows
        inbox = self.inbox[s]
        array = self.array
        def body(i, carry):
            at = pl.multiple_of(i * chunk, chunk)
            here = (pl.ds(pl.multiple_of(row + at, chunk), chunk), pl.ds(column, columns))
            total = array[here].astype(jnp.float32) + inbox[pl.ds(at, chunk), :].astype(jnp.float32)
            array[here] = total.astype(array.dtype)
            return carry
        lax.fori_loop(0, rows // chunk, body, 0)

    def share(self, s):
        if self.plan[s][1] != "full":
            pl.semaphore_wait(self.free.at[s], 1)
            self.share_copy(s).start()

    def collect(self, s):
        if self.plan[s][1] != "full":
            self.share_copy(s).wait()


HIGHEST = lax.Precision.HIGHEST
LANES = 128
PANEL = 2048

def ceil8(v):
    return -(-v // 8) * 8

def sin_cos(x):
    turns = jnp.round(x * (2.0 / math.pi))
    r = ((x - turns * 1.5703125) - turns * 4.837512969970703125e-4) - turns * 7.54978995489188e-8
    quadrant = turns.astype(jnp.int32)
    z = r * r
    s = ((-1.9515295891e-4 * z + 8.3321608736e-3) * z - 1.6666654611e-1) * z * r + r
    c = ((2.443315711809948e-5 * z - 1.388731625493765e-3) * z + 4.166664568298827e-2) * z * z - 0.5 * z + 1.0
    swap = (quadrant & 1) == 1
    sin_part = jnp.where(swap, c, s)
    cos_part = jnp.where(swap, s, c)
    sin_out = jnp.where((quadrant & 2) == 2, -sin_part, sin_part)
    cos_out = jnp.where(((quadrant + 1) & 2) == 2, -cos_part, cos_part)
    return sin_out, cos_out

def dot(a, b, ca, cb, precision=None):
    return lax.dot_general(a, b, (((ca,), (cb,)), ((), ())), precision=precision, preferred_element_type=jnp.float32)

class Sizes:
    def __init__(self, n, rows, local, width, emb, filt, hidden=3072):
        self.hidden, self.block = hidden, hidden // 8
        self.n, self.rows, self.local, self.width, self.emb, self.filt = n, rows, local, width, emb, filt
        self.length = n * local
        self.cpd = width // n
        self.cpad = ceil8(self.cpd)
        self.nb = self.length // LANES
        self.tokens = rows * local
        self.tiles = self.tokens // LANES
        self.erows = ceil8(emb)
        self.panel = min(PANEL, self.length)
        self.panels = self.length // self.panel
        assert local * 2 == LANES and rows == 4

def own_selection(z, me):
    want = lax.broadcasted_iota(jnp.int32, (z.cpad, z.width), 0)
    have = lax.broadcasted_iota(jnp.int32, (z.cpad, z.width), 1)
    return jnp.where((have == want + me * z.cpd) & (want < z.cpd), 1.0, 0.0).astype(jnp.float32)

def embed_rows(z, at, count):
    row = lax.broadcasted_iota(jnp.int32, (z.erows, count), 0)
    t = at + lax.broadcasted_iota(jnp.int32, (z.erows, count), 1)
    bands = (z.emb - 1) // 2
    harmonic = jnp.where(row <= bands, row, row - bands)
    angle = lax.rem(t * harmonic, z.length).astype(jnp.float32) * (2.0 * math.pi / z.length)
    s, c = sin_cos(angle)
    scaled = t.astype(jnp.float32) / z.length
    return jnp.where(row == 0, scaled, jnp.where(row <= bands, c, jnp.where(row < z.emb, s, 0.0)))

def columns(ref, count):
    eye = (lax.broadcasted_iota(jnp.int32, (count, count), 0) == lax.broadcasted_iota(jnp.int32, (count, count), 1)).astype(jnp.float32)
    return dot(eye, jnp.broadcast_to(ref[...], (8, count)), 1, 1, HIGHEST)[:, 0:1]

CHUNK = 512

def filter_setup(z, me, w, keep):
    select = own_selection(z, me)
    keep.own_filter[...] = dot(select, w.filter_weight[...], 1, 1, HIGHEST)
    own_decay = dot(select, jnp.broadcast_to(w.decay_rates[...], (8, z.width)), 1, 1, HIGHEST)[:, 0:1]
    keep.own_decay[...] = jnp.broadcast_to(own_decay, (z.cpad, LANES))
    keep.embed_pad[...] = jnp.zeros((z.erows, z.filt), jnp.float32)
    keep.embed_pad[0:z.emb, :] = w.embed_weight[...]
    keep.bias_one[...] = jnp.broadcast_to(columns(w.embed_bias, z.filt), (z.filt, LANES))
    keep.bias_two[...] = jnp.broadcast_to(columns(w.inner_bias, z.filt), (z.filt, LANES))


def filter_hidden(z, w, keep, at):
    embedded = embed_rows(z, at, CHUNK)
    s1, c1 = sin_cos(dot(keep.embed_pad[...], embedded, 0, 0, HIGHEST) + keep.bias_one[:, 0:1])
    s2, c2 = sin_cos(dot(w.inner_weight[...], s1, 0, 0, HIGHEST) + keep.bias_two[:, 0:1])
    scaled = (at + lax.broadcasted_iota(jnp.int32, (z.cpad, CHUNK), 1)).astype(jnp.float32) / z.length
    window = jnp.exp(-keep.own_decay[:, 0:1] * scaled)
    return embedded, s1, c1, s2, c2, scaled, window


def filter_forward(z, w, keep, begin, end):
    def body(i, carry):
        at = pl.multiple_of(i * CHUNK, CHUNK)
        embedded, s1, c1, s2, c2, scaled, window = filter_hidden(z, w, keep, at)
        keep.taps[:, pl.ds(at, CHUNK)] = dot(keep.own_filter[...], s2, 1, 0, HIGHEST) * window
        return carry
    lax.fori_loop(begin, end, body, 0)

def filter_backward(z, w, keep, grad_taps, sums):
    for ref in vars(sums).values():
        ref[...] = jnp.zeros(ref.shape, jnp.float32)
    def body(i, carry):
        at = pl.multiple_of(i * CHUNK, CHUNK)
        here = (slice(None), pl.ds(at, CHUNK))
        embedded, s1, c1, s2, c2, scaled, window = filter_hidden(z, w, keep, at)
        grad = grad_taps[here]
        decay = -jnp.sum(grad * keep.taps[here] * scaled, axis=1, keepdims=True)
        sums.decay[...] += jnp.broadcast_to(decay, (z.cpad, LANES))
        grad_raw = grad * window
        sums.filter[...] += dot(grad_raw, s2, 1, 1, HIGHEST)
        two = dot(keep.own_filter[...], grad_raw, 0, 0, HIGHEST) * c2
        sums.inner[...] += dot(s1, two, 1, 1, HIGHEST)
        sums.inner_bias[...] += jnp.broadcast_to(jnp.sum(two, axis=1, keepdims=True), (z.filt, LANES))
        one = dot(w.inner_weight[...], two, 1, 0, HIGHEST) * c1
        sums.embed[...] += dot(embedded, one, 1, 1, HIGHEST)
        sums.embed_bias[...] += jnp.broadcast_to(jnp.sum(one, axis=1, keepdims=True), (z.filt, LANES))
        return carry
    lax.fori_loop(0, z.length // CHUNK, body, 0)

def build_toeplitz(z, taps, pool):
    sub = lax.broadcasted_iota(jnp.int32, (8, z.length), 0)
    lane = lax.broadcasted_iota(jnp.int32, (8, LANES), 1)
    sub1 = lax.broadcasted_iota(jnp.int32, (8, LANES), 0)
    def body(c, carry):
        base = jnp.broadcast_to(taps[pl.ds(c, 1), :], (8, z.length))
        for bit in (1, 2, 4):
            base = jnp.where((sub & bit) == bit, pltpu.roll(base, bit, 1), base)
        for q in range(0, LANES // 8, 2):
            parts = []
            for u in (q, q + 1):
                part = pltpu.roll(base, 8 * u, 1) if u else base
                first = jnp.where(lane >= sub1 + 8 * u, part[:, :LANES], 0.0)
                parts.append(jnp.concatenate([first, part[:, LANES:]], axis=1))
            pair = jnp.concatenate(parts, axis=0).astype(jnp.bfloat16)
            for k in range(z.panels):
                at = pl.multiple_of((c * z.panels + k) * LANES, LANES) + 8 * q
                pool[pl.ds(pl.multiple_of(at, 16), 16), :] = pair[:, k * z.panel:(k + 1) * z.panel]
        return carry
    lax.fori_loop(0, z.cpd, body, 0)

def fold_panel(z, k, product, fold):
    lane = lax.broadcasted_iota(jnp.int32, (8, LANES), 1)
    row = lax.broadcasted_iota(jnp.int32, (8, LANES), 0)
    sums, before = None, None
    for u in range(LANES // 8):
        part = product[8 * u:8 * u + 8, :]
        first = part[:, :LANES]
        inside = lane >= row + 8 * u
        part = jnp.concatenate([jnp.where(inside, first, 0.0), part[:, LANES:]], axis=1)
        part = pltpu.roll(part, z.panel - 8 * u, 1) if u else part
        sums = part if sums is None else sums + part
        if k:
            outside = jnp.where(inside, 0.0, first)
            outside = pltpu.roll(outside, LANES - 8 * u, 1) if u else outside
            before = outside if before is None else before + outside
    fold[:, k * z.panel:(k + 1) * z.panel] = sums
    if k:
        fold[:, k * z.panel - LANES:k * z.panel] += before


def fold_rows(z, fold):
    sums = fold[...]
    row = lax.broadcasted_iota(jnp.int32, sums.shape, 0)
    for bit in (1, 2, 4):
        sums = jnp.where((row & bit) == bit, pltpu.roll(sums, z.length - bit, 1), sums)
    return jnp.sum(sums, axis=0, keepdims=True)

class Exchange:
    def __init__(self, outgoing, incoming, sends, arrivals, me, n):
        self.outgoing, self.incoming, self.sends, self.arrivals, self.me, self.n = outgoing, incoming, sends, arrivals, me, n
    def copy(self, k):
        to = lax.rem(self.me + k, self.n)
        return pltpu.make_async_remote_copy(
            src_ref=self.outgoing.at[to], dst_ref=self.incoming.at[self.me],
            send_sem=self.sends.at[k], recv_sem=self.arrivals.at[k],
            device_id=(to,), device_id_type=MESH)
    def start(self):
        def body(k, carry):
            self.copy(k).start()
            return carry
        lax.fori_loop(1, self.n, body, 0)
        self.incoming[self.me] = self.outgoing[self.me]
    def wait(self):
        def body(k, carry):
            self.copy(k).wait()
            return carry
        lax.fori_loop(1, self.n, body, 0)

def each_slab(z, body):
    if z.cpd % 8 == 0:
        lax.fori_loop(0, z.n, body, 0)
    else:
        for k in range(z.n):
            body(k, 0)

def slabs_from_rows(z, flipped, outgoing):
    def body(k, carry):
        at = k * z.cpd
        if z.cpd % 8 == 0:
            at = pl.multiple_of(at, 8)
        slab = flipped[pl.ds(at, z.cpad), :]
        outgoing[k] = jnp.concatenate([slab[:, :LANES], slab[:, LANES:]], axis=0).astype(outgoing.dtype)
        return carry
    each_slab(z, body)

def rows_from_slabs(z, incoming, flipped):
    def body(k, carry):
        at = k * z.cpd
        if z.cpd % 8 == 0:
            at = pl.multiple_of(at, 8)
        slab = incoming[k].astype(jnp.float32)
        flipped[pl.ds(at, z.cpad), :] = jnp.concatenate([slab[:z.cpad], slab[z.cpad:]], axis=1)
        return carry
    each_slab(z, body)

def widen_slabs(z, incoming, wide):
    def body(j, carry):
        wide[pl.ds(pl.multiple_of(j * 2 * z.cpad, 8), 2 * z.cpad), :] = incoming[j].astype(jnp.float32)
        return carry
    lax.fori_loop(0, z.n, body, 0)

def narrow_slabs(z, wide, outgoing):
    def body(j, carry):
        outgoing[j] = wide[pl.ds(pl.multiple_of(j * 2 * z.cpad, 8), 2 * z.cpad), :].astype(outgoing.dtype)
        return carry
    lax.fori_loop(0, z.n, body, 0)

def channel_blocks(z, wide, c):
    lane = lax.broadcasted_iota(jnp.int32, (z.nb, LANES), 1)
    low = lane < LANES // 2
    out = []
    for t in range(2):
        even = wide[pl.ds(t * z.cpad + c, z.nb, 4 * z.cpad), :]
        odd = wide[pl.ds((2 + t) * z.cpad + c, z.nb, 4 * z.cpad), :]
        out.append(jnp.where(low, even, pltpu.roll(odd, LANES // 2, 1)))
        out.append(jnp.where(low, pltpu.roll(even, LANES // 2, 1), odd))
    return out

def put_channel_blocks(z, wide, c, blocks):
    lane = lax.broadcasted_iota(jnp.int32, (z.nb, LANES), 1)
    low = lane < LANES // 2
    for t in range(2):
        a, b = blocks[2 * t], blocks[2 * t + 1]
        wide[pl.ds(t * z.cpad + c, z.nb, 4 * z.cpad), :] = jnp.where(low, a, pltpu.roll(b, LANES // 2, 1))
        wide[pl.ds((2 + t) * z.cpad + c, z.nb, 4 * z.cpad), :] = jnp.where(low, pltpu.roll(a, LANES // 2, 1), b)

def panel_rows(z, c, k):
    return pl.ds(pl.multiple_of((c * z.panels + k) * LANES, LANES), LANES)


def convolve_forward(z, wide, pool, kept, spread):
    each = z.panel // LANES
    def body(c, carry):
        blocks = channel_blocks(z, wide, c)
        x = jnp.concatenate(blocks, axis=0).astype(jnp.bfloat16)
        kept[c] = x
        spread[...] = jnp.zeros(spread.shape, jnp.float32)
        for k in range(z.panels):
            product = dot(x, pool[panel_rows(z, c, k), :], 1, 0)
            for i in range(each):
                d = k * each + i
                for r in range(4):
                    spread[r, d:d + z.nb, :] += product[r * z.nb:(r + 1) * z.nb, i * LANES:(i + 1) * LANES]
        put_channel_blocks(z, wide, c, [spread[r, 0:z.nb, :] for r in range(4)])
        return carry
    lax.fori_loop(0, z.cpd, body, 0)


def convolve_back_channel(z, c, wide, panel_of, kept, spread, advanced, back, fold, grad_taps):
    blocks = channel_blocks(z, wide, c)
    for r in range(4):
        spread[r, 0:z.nb, :] = blocks[r]
    each = z.panel // LANES
    source = kept[c].astype(jnp.float32).T.astype(jnp.bfloat16)
    for k in range(z.panels):
        for i in range(each):
            d = k * each + i
            advanced[:, i * LANES:(i + 1) * LANES] = jnp.concatenate(
                [spread[r, d:d + z.nb, :] for r in range(4)], axis=0).astype(jnp.bfloat16)
        panel = panel_of(c, k)
        product = dot(advanced[...], panel[...], 1, 1)
        back[...] = product if k == 0 else back[...] + product
        fold_panel(z, k, dot(source, advanced[...], 1, 0), fold)
    put_channel_blocks(z, wide, c, [back[r * z.nb:(r + 1) * z.nb, :] for r in range(4)])
    grad_taps[pl.ds(c, 1), :] = fold_rows(z, fold)


class Names:
    def __init__(self, names, values):
        vars(self).update(zip(names, values))


def keep_shapes(z):
    return dict(
        own_filter=(z.cpad, z.filt), own_decay=(z.cpad, LANES), embed_pad=(z.erows, z.filt),
        bias_one=(z.filt, LANES), bias_two=(z.filt, LANES), taps=(z.cpad, z.length),
    )


def sum_shapes(z):
    return dict(
        decay=(z.cpad, LANES), filter=(z.cpad, z.filt), inner=(z.filt, z.filt), inner_bias=(z.filt, LANES),
        embed=(z.erows, z.filt), embed_bias=(z.filt, LANES),
    )


F32, BF16 = jnp.float32, jnp.bfloat16
BLOCKS = 8
WIDE = 256


class Row:
    FIRST_GAIN, FIRST_SHIFT, INPUT_BIAS, SHORT_KERNEL, SHORT_BIAS = 0, 1, 2, 5, 14
    DECAY, FILTER_BIAS, OUTPUT_BIAS, SECOND_GAIN, SECOND_SHIFT, UP_BIAS, DOWN_BIAS = 17, 18, 19, 20, 21, 22, 26
    EMBED_BIAS, INNER_BIAS = 27, 28
    FILTER, NETWORK, TOTAL = 32, 96, 128


def normalize(x):
    center = x - jnp.mean(x, axis=-1, keepdims=True)
    inverse = lax.rsqrt(jnp.mean(center * center, axis=-1, keepdims=True) + EPSILON)
    return center * inverse, inverse


def normalize_back(gradient, gain, unit, inverse):
    q = gradient * gain
    return (q - jnp.mean(q, axis=-1, keepdims=True) - unit * jnp.mean(q * unit, axis=-1, keepdims=True)) * inverse


def as_row(column):
    size = column.shape[0]
    row, lane = (lax.broadcasted_iota(jnp.int32, (size, size), i) for i in range(2))
    return dot(column, jnp.where(row == lane, 1.0, 0.0).astype(F32), 0, 0, HIGHEST)[0:1, :]


def total(x):
    return jnp.sum(x, axis=0, keepdims=True)


def row_masks(z, me, lengths, keep_one, keep_two):
    for r in range(z.rows):
        position = me * z.local + lax.broadcasted_iota(jnp.int32, (z.local, LANES), 0)
        first = position == 0
        second = position == 1
        end = 0
        for j in range(lengths.shape[1] - 1):
            end = end + lengths[r, j]
            first = first | (position == end)
            second = second | (position == end + 1)
        keep_one[r * z.local:(r + 1) * z.local, :] = jnp.where(first, 0.0, 1.0)
        keep_two[r * z.local:(r + 1) * z.local, :] = jnp.where(first | second, 0.0, 1.0)


def lagged(z, values, halo, t, columns):
    row = lax.broadcasted_iota(jnp.int32, (LANES, 1), 0)
    one, two = pltpu.roll(values, 1, 0), pltpu.roll(values, 2, 0)
    for u in range(2):
        r = 2 * t + u
        older, newer = halo[2 * r:2 * r + 1, columns], halo[2 * r + 1:2 * r + 2, columns]
        one = jnp.where(row == u * z.local, newer, one)
        two = jnp.where(row == u * z.local, older, jnp.where(row == u * z.local + 1, newer, two))
    return one, two


def halves(t):
    return slice(t * LANES, (t + 1) * LANES)


class Flow:
    def __init__(self, reduction):
        self.reduction = reduction
        self.steps = len(reduction.plan)
        self.at = -1
    def advance(self):
        s, n, r = self.at, self.steps, self.reduction
        if s < 0:
            r.give(0)
        elif s < n - 1:
            r.take(s)
            r.give(s + 1)
        elif s == n - 1:
            r.take(s)
            r.share(s)
        elif s < 2 * n - 1:
            r.collect(2 * n - 1 - s)
            r.share(2 * n - 2 - s)
        elif s == 2 * n - 1:
            r.collect(0)
        self.at += 1
    @property
    def done(self):
        return self.at >= 2 * self.steps


def advance(*flows):
    for flow in flows:
        if not flow.done:
            flow.advance()


def block_kernel(z, order, schedule, *refs):
    inputs, outs, scratch, fetched, keep_names, sum_names = order
    v = Names(inputs + outs + scratch, refs)
    me = lax.axis_index("seq")
    n = z.n
    d = z.width
    p = Names(fetched, [getattr(v, "v_" + name) for name in fetched])
    def fetch(name):
        source, target = getattr(v, name), getattr(p, name)
        if len(source.shape) == 1:
            target = target.at[0]
        return pltpu.make_async_copy(source, target, v.loads.at[fetched.index(name)])
    late = ("input_weight", "output_weight", "cotangent")
    soon = [name for name in fetched if name not in late]
    for name in soon + list(late):
        fetch(name).start()
    def weight_block(j, slot):
        at = pl.multiple_of(j * z.block, LANES)
        return (
            pltpu.make_async_copy(v.up_weight.at[:, pl.ds(at, z.block)], v.up_slots.at[slot], v.stream.at[0, slot]),
            pltpu.make_async_copy(v.down_weight.at[pl.ds(at, z.block), :], v.down_slots.at[slot], v.stream.at[1, slot]),
        )
    for copy in weight_block(0, 0):
        copy.start()
    barrier = pltpu.get_barrier_semaphore()
    def greet(k, carry):
        pl.semaphore_signal(barrier, inc=1, device_id=(lax.rem(me + k, n),), device_id_type=MESH)
        return carry
    lax.fori_loop(1, n, greet, 0)
    small = v.g_small
    small[0:Row.FILTER, :] = jnp.zeros((Row.FILTER, d), F32)
    small[Row.NETWORK:Row.TOTAL, :] = jnp.zeros((Row.TOTAL - Row.NETWORK, d), F32)
    row_masks(z, me, v.doc_lengths, v.keep_one, v.keep_two)

    for name in soon:
        fetch(name).wait()
    tokens = p.tokens
    for t in range(z.tiles):
        unit, inverse = normalize(tokens[halves(t), :].astype(F32))
        v.unit_one[halves(t), :] = unit
        v.inverse_one[halves(t), :] = jnp.broadcast_to(inverse, (LANES, LANES))
        v.normed[halves(t), :] = (unit * p.first_gain[...] + p.first_shift[...]).astype(BF16)
    fetch("input_weight").wait()
    part = 3 * d // 6
    def project(j, carry):
        here = pl.ds(pl.multiple_of(j * part, LANES), part)
        values = (dot(v.normed[...], p.input_weight[:, here], 1, 0) + p.input_bias[:, here]).astype(BF16)
        v.projected[:, here] = values
        rounded = values.astype(F32)
        for r in range(z.rows):
            last = (r + 1) * z.local
            v.rim_out[2 * r:2 * r + 2, here] = rounded[last - 2:last, :]
        return carry
    lax.fori_loop(0, 6, project, 0)
    pl.semaphore_wait(barrier, n - 1)
    ahead, behind = lax.rem(me + 1, n), lax.rem(me + n - 1, n)
    rim = pltpu.make_async_remote_copy(
        src_ref=v.rim_out, dst_ref=v.rim_in, send_sem=v.rims.at[0], recv_sem=v.rims.at[1],
        device_id=(ahead,), device_id_type=MESH)
    rim.start()
    keep = Names(keep_names, [getattr(v, "k_" + name) for name in keep_names])
    chunks = z.length // CHUNK
    early = chunks // 2
    filter_setup(z, me, p, keep)
    filter_forward(z, p, keep, 0, early)
    rim.wait()

    def short(j, carry):
        inner = pl.ds(pl.multiple_of(j * WIDE, LANES), WIDE)
        for t in range(z.tiles):
            k1, k2 = v.keep_one[halves(t), 0:1], v.keep_two[halves(t), 0:1]
            streams = []
            for s in range(3):
                here = pl.ds(pl.multiple_of(s * d + j * WIDE, LANES), WIDE)
                values = v.projected[halves(t), here].astype(F32)
                one, two = lagged(z, values, v.rim_in, t, here)
                taps = p.short_kernel
                out = (taps[0:1, here] * values + taps[1:2, here] * (k1 * one) + taps[2:3, here] * (k2 * two)
                       + p.short_bias[:, here])
                (v.gate_zero, v.gate_one, v.value_part)[s][halves(t), inner] = out
                streams.append(out)
            v.flipped[inner, halves(t)] = (streams[1] * streams[2]).T
        return carry
    lax.fori_loop(0, d // WIDE, short, 0)
    v.flipped[d:, :] = jnp.zeros((8, z.tokens), F32)

    def exchange(i):
        return Exchange(v.slabs_out.at[i % 2], v.slabs_in.at[i % 2], v.sends.at[i], v.arrivals.at[i], me, n)
    slabs_from_rows(z, v.flipped, v.slabs_out.at[0])
    first = exchange(0)
    first.start()
    filter_forward(z, p, keep, early, chunks)
    build_toeplitz(z, keep.taps, v.pool)
    first.wait()
    widen_slabs(z, v.slabs_in.at[0], v.wide)
    save = pltpu.make_async_copy(v.pool, v.toeplitz_saved, v.saves.at[0])
    save.start()
    convolve_forward(z, v.wide, v.pool, v.kept, v.spread)
    save.wait()
    narrow_slabs(z, v.wide, v.slabs_out.at[1])
    second = exchange(1)
    second.start()
    fetch("output_weight").wait()
    fetch("cotangent").wait()
    cotangent = p.cotangent
    small[Row.DOWN_BIAS:Row.DOWN_BIAS + 1, :] = total(cotangent[...].astype(F32))
    second.wait()
    rows_from_slabs(z, v.slabs_in.at[1], v.flipped)

    def gate(j, carry):
        inner = pl.ds(pl.multiple_of(j * WIDE, LANES), WIDE)
        for t in range(z.tiles):
            gated = v.value_part[halves(t), inner] * v.gate_one[halves(t), inner]
            conv = v.flipped[inner, halves(t)].T + p.filter_bias[:, inner] * gated
            v.conv[halves(t), inner] = conv
            v.mixed[halves(t), inner] = (conv * v.gate_zero[halves(t), inner]).astype(BF16)
        return carry
    lax.fori_loop(0, d // WIDE, gate, 0)
    for t in range(z.tiles):
        branch = dot(v.mixed[halves(t), :], p.output_weight[...], 1, 0) + p.output_bias[...]
        residual = tokens[halves(t), :].astype(F32) + branch
        unit, inverse = normalize(residual)
        v.unit_two[halves(t), :] = unit
        v.inverse_two[halves(t), :] = jnp.broadcast_to(inverse, (LANES, LANES))
        v.normed_two[halves(t), :] = (unit * p.second_gain[...] + p.second_shift[...]).astype(BF16)
        v.residual[halves(t), :] = residual + p.down_bias[...]
    v.grad_normed[...] = jnp.zeros((z.tokens, d), F32)

    flows = {}
    for name in PARTS:
        inboxes = part_inboxes(z, v, name)
        flows[name] = Flow(Reduction(getattr(v, "g_" + name), z.plans[name], inboxes, getattr(v, "sends_" + name), getattr(v, "arrivals_" + name), getattr(v, "free_" + name), me))

    def mlp(j, down_grad, up_grad, first_block):
        slot = lax.rem(j, 2)
        for copy in weight_block(j, slot):
            copy.wait()
        @pl.when(j + 1 < BLOCKS)
        def _():
            for copy in weight_block(j + 1, 1 - slot):
                copy.start()
        up, down = v.up_slots[slot], v.down_slots[slot]
        here = pl.ds(pl.multiple_of(j * z.block, LANES), z.block)
        local = j - first_block
        x = dot(v.normed_two[...], up, 1, 0) + p.up_bias[:, here]
        grad_hidden = dot(cotangent[...], down, 1, 1)
        root = math.sqrt(2.0 / math.pi)
        square = x * x
        curve = jnp.tanh(root * (x + 0.044715 * (square * x)))
        half = 0.5 * (1.0 + curve)
        hidden = (x * half).astype(BF16)
        slope = half + 0.5 * x * (1.0 - curve * curve) * (root * (1.0 + 3.0 * 0.044715 * square))
        grad_pre = (grad_hidden * slope).astype(BF16)
        v.residual[...] += dot(hidden, down, 1, 0)
        v.grad_normed[...] += dot(grad_pre, up, 1, 1)
        down_grad[pl.ds(pl.multiple_of(local * z.block, LANES), z.block), :] = dot(hidden, cotangent[...], 0, 0).astype(BF16)
        up_grad[:, pl.ds(pl.multiple_of(local * z.block, LANES), z.block)] = dot(v.normed_two[...], grad_pre, 0, 0).astype(BF16)
        v.up_sums[:, here] = total(grad_pre.astype(F32))
    def mlp_half(k):
        def body(j, carry):
            mlp(j, getattr(v, "g_down" + str(k)), getattr(v, "g_up" + str(k)), k * BLOCKS // 2)
            return carry
        lax.fori_loop(k * BLOCKS // 2, (k + 1) * BLOCKS // 2, body, 0)
    mlp_half(0)
    advance(flows["down0"], flows["up0"])
    mlp_half(1)
    advance(flows["down1"], flows["up1"])
    wide_rows = v.up_sums.shape[1] // d
    for i in range(wide_rows):
        small[Row.UP_BIAS + i:Row.UP_BIAS + i + 1, :] = v.up_sums[:, i * d:(i + 1) * d]
    v.normed_two[...] = v.residual[...].astype(BF16)
    store_out = pltpu.make_async_copy(v.normed_two, v.output, v.saves.at[1])
    store_out.start()

    gain_sum, shift_sum, bias_sum = 0.0, 0.0, 0.0
    for t in range(z.tiles):
        gradient = v.grad_normed[halves(t), :]
        unit = v.unit_two[halves(t), :]
        gain_sum = gain_sum + total(gradient * unit)
        shift_sum = shift_sum + total(gradient)
        value = cotangent[halves(t), :].astype(F32) + normalize_back(gradient, p.second_gain[...], unit, v.inverse_two[halves(t), 0:1])
        v.residual[halves(t), :] = value
        branch = value.astype(BF16)
        v.grad_branch[halves(t), :] = branch
        bias_sum = bias_sum + total(branch.astype(F32))
    small[Row.SECOND_GAIN:Row.SECOND_GAIN + 1, :] = gain_sum
    small[Row.SECOND_SHIFT:Row.SECOND_SHIFT + 1, :] = shift_sum
    small[Row.OUTPUT_BIAS:Row.OUTPUT_BIAS + 1, :] = bias_sum
    grad_conv, grad_gate_zero = v.unit_two, v.grad_normed
    def mix_back(j, carry):
        inner = pl.ds(pl.multiple_of(j * WIDE, LANES), WIDE)
        sums = jnp.zeros((1, WIDE), F32)
        for t in range(z.tiles):
            grad_mixed = dot(v.grad_branch[halves(t), :], p.output_weight[inner, :], 1, 1)
            back = grad_mixed * v.gate_zero[halves(t), inner]
            grad_conv[halves(t), inner] = back
            grad_gate_zero[halves(t), inner] = grad_mixed * v.conv[halves(t), inner]
            gated = v.value_part[halves(t), inner] * v.gate_one[halves(t), inner]
            sums = sums + total(back * gated)
            v.flipped[inner, halves(t)] = back.T
        small[Row.FILTER_BIAS:Row.FILTER_BIAS + 1, inner] = sums
        return carry
    lax.fori_loop(0, d // WIDE, mix_back, 0)
    slabs_from_rows(z, v.flipped, v.slabs_out.at[0])
    third = exchange(2)
    third.start()
    def load_panel(i):
        saved = v.toeplitz_saved.at[pl.ds(pl.multiple_of(i * LANES, LANES), LANES), :]
        slot = lax.rem(i, 2)
        return pltpu.make_async_copy(saved, v.toeplitz_slots.at[slot], v.stream.at[2, slot])
    load_panel(0).start()
    def panel_of(c, k):
        i = c * z.panels + k
        load_panel(i).wait()
        @pl.when(i + 1 < z.cpd * z.panels)
        def _():
            load_panel(i + 1).start()
        return v.toeplitz_slots.at[lax.rem(i, 2)]
    def out_grad(j, carry):
        inner = pl.ds(pl.multiple_of(j * WIDE, LANES), WIDE)
        v.g_out[:, inner] = dot(v.mixed[...], v.grad_branch[:, inner], 0, 0).astype(BF16)
        return carry
    lax.fori_loop(0, d // WIDE, out_grad, 0)
    def run(step):
        for name in schedule.get(step, ()):
            advance(flows[name])
    run("start")
    third.wait()
    widen_slabs(z, v.slabs_in.at[0], v.wide)
    v.spread[...] = jnp.zeros(v.spread.shape, F32)
    v.grad_taps[...] = jnp.zeros(v.grad_taps.shape, F32)
    pieces = 4
    bounds = [z.cpd * i // pieces for i in range(pieces + 1)]
    def back_channel(c, carry):
        convolve_back_channel(z, c, v.wide, panel_of, v.kept, v.spread, v.advanced, v.back, v.fold, v.grad_taps)
        return carry
    for i in range(pieces):
        lax.fori_loop(bounds[i], bounds[i + 1], back_channel, 0)
        run("piece%d" % i)
    narrow_slabs(z, v.wide, v.slabs_out.at[1])
    fourth = exchange(3)
    fourth.start()
    run("sent")
    sums = Names(sum_names, [getattr(v, "s_" + name) for name in sum_names])
    filter_backward(z, p, keep, v.grad_taps, sums)
    select = own_selection(z, me)
    small[Row.FILTER:Row.NETWORK, :] = dot(sums.filter[...], select, 0, 0, HIGHEST)
    small[Row.DECAY:Row.DECAY + 1, :] = dot(sums.decay[...], select, 0, 0, HIGHEST)[0:1, :]
    half = z.filt // 2
    small[Row.NETWORK:Row.NETWORK + half, 0:z.filt] = sums.inner[0:half, :]
    small[Row.NETWORK:Row.NETWORK + half, LANES:LANES + z.filt] = sums.inner[half:, :]
    small[Row.NETWORK:Row.NETWORK + half, 2 * LANES:2 * LANES + z.filt] = sums.embed[0:half, :]
    small[Row.NETWORK:Row.NETWORK + z.erows - half, 3 * LANES:3 * LANES + z.filt] = sums.embed[half:, :]
    small[Row.EMBED_BIAS:Row.EMBED_BIAS + 1, 0:z.filt] = as_row(sums.embed_bias[...])
    small[Row.INNER_BIAS:Row.INNER_BIAS + 1, 0:z.filt] = as_row(sums.inner_bias[...])
    run("filter")
    fourth.wait()
    rows_from_slabs(z, v.slabs_in.at[1], v.flipped)
    run("back")

    def gate_back(j, carry):
        inner = pl.ds(pl.multiple_of(j * WIDE, LANES), WIDE)
        for t in range(z.tiles):
            grad_gated = v.flipped[inner, halves(t)].T + p.filter_bias[:, inner] * grad_conv[halves(t), inner]
            first_part = grad_gated * v.value_part[halves(t), inner]
            second_part = grad_gated * v.gate_one[halves(t), inner]
            v.gate_one[halves(t), inner] = first_part
            v.value_part[halves(t), inner] = second_part
            for s, value in enumerate((grad_gate_zero[halves(t), inner], first_part, second_part)):
                here = pl.ds(pl.multiple_of(s * d + j * WIDE, LANES), WIDE)
                taps = p.short_kernel
                for u in range(2):
                    r = 2 * t + u
                    lo = u * z.local
                    head = value[lo:lo + 8, :]
                    one = (taps[1:2, here] * v.keep_one[r * z.local:r * z.local + 8, 0:1]) * head
                    two = (taps[2:3, here] * v.keep_two[r * z.local:r * z.local + 8, 0:1]) * head
                    v.rim_back_out[2 * r:2 * r + 1, here] = two[0:1]
                    v.rim_back_out[2 * r + 1:2 * r + 2, here] = one[0:1] + two[1:2]
        return carry
    lax.fori_loop(0, d // WIDE, gate_back, 0)
    rim_back = pltpu.make_async_remote_copy(
        src_ref=v.rim_back_out, dst_ref=v.rim_back_in, send_sem=v.rims.at[2], recv_sem=v.rims.at[3],
        device_id=(behind,), device_id_type=MESH)
    rim_back.start()
    grad_streams = (grad_gate_zero, v.gate_one, v.value_part)
    def short_sums(j, carry):
        inner = pl.ds(pl.multiple_of(j * WIDE, LANES), WIDE)
        for s in range(3):
            here = pl.ds(pl.multiple_of(s * d + j * WIDE, LANES), WIDE)
            acc = [jnp.zeros((1, WIDE), F32)] * 4
            for t in range(z.tiles):
                k1, k2 = v.keep_one[halves(t), 0:1], v.keep_two[halves(t), 0:1]
                values = v.projected[halves(t), here].astype(F32)
                one, two = lagged(z, values, v.rim_in, t, here)
                value = grad_streams[s][halves(t), inner]
                acc[0] = acc[0] + total(value * values)
                acc[1] = acc[1] + total(value * (k1 * one))
                acc[2] = acc[2] + total(value * (k2 * two))
                acc[3] = acc[3] + total(value)
            for i in range(3):
                small[Row.SHORT_KERNEL + 3 * i + s:Row.SHORT_KERNEL + 3 * i + s + 1, inner] = acc[i]
            small[Row.SHORT_BIAS + s:Row.SHORT_BIAS + s + 1, inner] = acc[3]
        return carry
    lax.fori_loop(0, d // WIDE, short_sums, 0)
    run("short")
    rim_back.wait()
    def spread_back(j, carry):
        inner = pl.ds(pl.multiple_of(j * WIDE, LANES), WIDE)
        row = lax.broadcasted_iota(jnp.int32, (LANES, 1), 0)
        for s in range(3):
            here = pl.ds(pl.multiple_of(s * d + j * WIDE, LANES), WIDE)
            taps = p.short_kernel
            sums = jnp.zeros((1, WIDE), F32)
            for t in range(z.tiles):
                k1, k2 = v.keep_one[halves(t), 0:1], v.keep_two[halves(t), 0:1]
                value = grad_streams[s][halves(t), inner]
                one = pltpu.roll((taps[1:2, here] * k1) * value, LANES - 1, 0)
                two = pltpu.roll((taps[2:3, here] * k2) * value, LANES - 2, 0)
                later = one + two
                for u in range(2):
                    r = 2 * t + u
                    last = (u + 1) * z.local - 1
                    far, near = v.rim_back_in[2 * r:2 * r + 1, here], v.rim_back_in[2 * r + 1:2 * r + 2, here]
                    later = jnp.where(row == last, near, jnp.where(row == last - 1, one + far, later))
                low = (taps[0:1, here] * value + later).astype(BF16)
                v.projected[halves(t), here] = low
                sums = sums + total(low.astype(F32))
            small[Row.INPUT_BIAS + s:Row.INPUT_BIAS + s + 1, inner] = sums
        return carry
    lax.fori_loop(0, d // WIDE, spread_back, 0)
    run("spread")
    for k in range(2):
        width = 3 * d // 2
        step = width // 3
        def in_grad(j, carry, k=k):
            here = pl.ds(pl.multiple_of(k * width + j * step, LANES), step)
            there = pl.ds(pl.multiple_of(j * step, LANES), step)
            getattr(v, "g_in" + str(k))[:, there] = dot(v.normed[...], v.projected[:, here], 0, 0).astype(BF16)
            return carry
        lax.fori_loop(0, 3, in_grad, 0)
        advance(flows["in" + str(k)])
    v.conv[...] = jnp.zeros((z.tokens, d), F32)
    def norm_grad(j, carry):
        here = pl.ds(pl.multiple_of(j * part, LANES), part)
        v.conv[...] += dot(v.projected[:, here], p.input_weight[:, here], 1, 1)
        return carry
    lax.fori_loop(0, 6, norm_grad, 0)
    gain_sum, shift_sum = 0.0, 0.0
    store_out.wait()
    for t in range(z.tiles):
        gradient = v.conv[halves(t), :]
        unit = v.unit_one[halves(t), :]
        gain_sum = gain_sum + total(gradient * unit)
        shift_sum = shift_sum + total(gradient)
        value = v.residual[halves(t), :] + normalize_back(gradient, p.first_gain[...], unit, v.inverse_one[halves(t), 0:1])
        v.normed_two[halves(t), :] = value.astype(BF16)
    store_grad = pltpu.make_async_copy(v.normed_two, v.grad_tokens, v.saves.at[2])
    store_grad.start()
    small[Row.FIRST_GAIN:Row.FIRST_GAIN + 1, :] = gain_sum
    small[Row.FIRST_SHIFT:Row.FIRST_SHIFT + 1, :] = shift_sum
    advance(flows["small"])

    stored = {}
    def finish(name):
        flow = flows[name]
        if not flow.done:
            flow.advance()
        if flow.done and name not in stored:
            stored[name] = pltpu.make_async_copy(getattr(v, "g_" + name), getattr(v, "r_" + name), v.saves.at[3 + PARTS.index(name)])
            stored[name].start()
    for names in schedule["tail"]:
        for name in names:
            finish(name)
    while len(stored) < len(PARTS):
        for name in PARTS:
            finish(name)
    for copy in stored.values():
        copy.wait()
    store_grad.wait()


PARTS = ("down0", "up0", "down1", "up1", "out", "in0", "in1", "small")


def part_shapes(z):
    d, f = z.width, z.hidden
    return {
        "down0": ((f // 2, d), BF16), "down1": ((f // 2, d), BF16), "up0": ((d, f // 2), BF16), "up1": ((d, f // 2), BF16),
        "out": ((d, d), BF16), "in0": ((d, 3 * d // 2), BF16), "in1": ((d, 3 * d // 2), BF16), "small": ((Row.TOTAL, d), F32),
    }


def part_plans(z):
    bits = []
    bit = 1
    while bit < z.n:
        bits.append(bit)
        bit *= 2
    core, x, y, rest = bits[:1], bits[1:2], bits[2:3], bits[3:]
    first = core + x + rest[:1] + y + rest[1:]
    second = core + y + rest[:1] + x + rest[1:]
    orders = {"down0": first, "down1": first, "up0": second, "up1": second, "out": first, "in0": first, "in1": second, "small": second}
    shapes = part_shapes(z)
    plans = {}
    for name in PARTS:
        (rows, columns), kind = shapes[name]
        plans[name] = halving_plan(rows, columns, orders[name], 8 if kind == F32 else 16)
    return plans


POOLED = ("up0", "up1", "down0", "down1")


def part_inboxes(z, v, name):
    if name not in POOLED:
        return [getattr(v, "inbox_%s_%d" % (name, s)) for s in range(len(z.plans[name]))]
    d = z.width
    index = POOLED.index(name)
    views = []
    row, column = (index * d, 0) if index < 2 else (2 * d, (index - 2) * d)
    whole = part_shapes(z)[name][0][1]
    for _, _, rows, columns in z.plans[name]:
        views.append(v.pool.at[pl.ds(row, rows), pl.ds(column, columns)])
        if columns == whole:
            row += rows
        else:
            column += columns
    return views


def block(z, inputs, collective_id=0):
    d, f = z.width, z.hidden
    shapes = part_shapes(z)
    keep = keep_shapes(z)
    sums = sum_shapes(z)
    names, specs = [], []
    any_space = pl.BlockSpec(memory_space=pl.ANY)
    for name in inputs:
        names.append(name)
        specs.append(pl.BlockSpec(memory_space=pltpu.SMEM) if name == "doc_lengths" else any_space)
    outs = dict(output=((z.tokens, d), BF16), grad_tokens=((z.tokens, d), BF16))
    for name in PARTS:
        outs["r_" + name] = shapes[name]
    pool = (z.cpd * z.panels * LANES, z.panel)
    outs["toeplitz_saved"] = (pool, BF16)
    scratch = {}
    fetched = tuple(name for name in inputs if name not in ("doc_lengths", "up_weight", "down_weight"))
    for name in fetched:
        shape = inputs[name].shape
        scratch["v_" + name] = pltpu.VMEM(shape if len(shape) > 1 else (1,) + shape, inputs[name].dtype)
    t = z.tokens
    buffers = dict(
        unit_one=((t, d), F32), inverse_one=((t, LANES), F32), normed=((t, d), BF16), projected=((t, 3 * d), BF16),
        rim_out=((8, 3 * d), F32), rim_in=((8, 3 * d), F32), rim_back_out=((8, 3 * d), F32), rim_back_in=((8, 3 * d), F32),
        keep_one=((t, LANES), F32), keep_two=((t, LANES), F32),
        gate_zero=((t, d), F32), gate_one=((t, d), F32), value_part=((t, d), F32),
        flipped=((d + 8, t), F32), slabs_out=((2, z.n, 2 * z.cpad, LANES), BF16), slabs_in=((2, z.n, 2 * z.cpad, LANES), BF16),
        wide=((z.n * 2 * z.cpad, LANES), F32), spread=((4, 2 * z.nb, LANES), F32), kept=((z.cpd, 4 * z.nb, LANES), BF16),
        pool=(pool, BF16),
        conv=((t, d), F32), mixed=((t, d), BF16), unit_two=((t, d), F32), inverse_two=((t, LANES), F32),
        normed_two=((t, d), BF16), residual=((t, d), F32), grad_normed=((t, d), F32),
        up_slots=((2, d, z.block), BF16), down_slots=((2, z.block, d), BF16), up_sums=((1, f), F32),
        grad_branch=((t, d), BF16), toeplitz_slots=((2, LANES, z.panel), BF16), back=((4 * z.nb, LANES), F32), fold=((8, z.length), F32),
        advanced=((4 * z.nb, z.panel), BF16), grad_taps=((z.cpad, z.length), F32),
    )
    for name, (shape, kind) in buffers.items():
        scratch[name] = pltpu.VMEM(shape, kind)
    for name in keep:
        scratch["k_" + name] = pltpu.VMEM(keep[name], F32)
    for name in sums:
        scratch["s_" + name] = pltpu.VMEM(sums[name], F32)
    for name in PARTS:
        scratch["g_" + name] = pltpu.VMEM(*shapes[name])
        if name not in POOLED:
            for s, (_, _, rows, columns) in enumerate(z.plans[name]):
                scratch["inbox_%s_%d" % (name, s)] = pltpu.VMEM((rows, columns), shapes[name][1])
        steps = len(z.plans[name])
        scratch["sends_" + name] = pltpu.SemaphoreType.DMA((2 * steps,))
        scratch["arrivals_" + name] = pltpu.SemaphoreType.DMA((2 * steps,))
        scratch["free_" + name] = pltpu.SemaphoreType.REGULAR((steps,))
    scratch["loads"] = pltpu.SemaphoreType.DMA((len(fetched),))
    scratch["stream"] = pltpu.SemaphoreType.DMA((3, 2))
    scratch["saves"] = pltpu.SemaphoreType.DMA((3 + len(PARTS),))
    scratch["rims"] = pltpu.SemaphoreType.DMA((4,))
    scratch["sends"] = pltpu.SemaphoreType.DMA((4, z.n))
    scratch["arrivals"] = pltpu.SemaphoreType.DMA((4, z.n))
    order = (tuple(names), tuple(outs), tuple(scratch), fetched, tuple(keep), tuple(sums))
    results = pl.pallas_call(
        functools.partial(block_kernel, z, order, SCHEDULE),
        out_shape=[jax.ShapeDtypeStruct(*outs[name]) for name in outs],
        in_specs=specs, out_specs=[any_space] * len(outs),
        scratch_shapes=list(scratch.values()),
        compiler_params=pltpu.CompilerParams(collective_id=collective_id, has_side_effects=True, vmem_limit_bytes=61 << 20),
        name="hyena_block",
    )(*inputs.values())
    return dict(zip(outs, results))


SCHEDULE = {
    "start": ("down0", "up0", "out", "down1", "up1"),
    "piece0": ("out",),
    "piece1": ("down0", "up0", "out"),
    "piece2": ("down1", "up1"),
    "piece3": ("down0", "up0", "out"),
    "sent": ("down1", "up1"),
    "filter": ("down0", "up0", "out"),
    "back": ("down1", "up1"),
    "short": ("down0", "up0", "out"),
    "spread": ("down1", "up1"),
    "tail": (),
}


def finish_layout(z):
    d, f = z.width, z.hidden
    return dict(
        grad_down_weight=((f, d), [("down0", 0, 0), ("down1", f // 2, 0)]),
        grad_up_weight=((d, f), [("up0", 0, 0), ("up1", 0, f // 2)]),
        grad_output_weight=((d, d), [("out", 0, 0)]),
        grad_input_weight=((d, 3 * d), [("in0", 0, 0), ("in1", 0, 3 * d // 2)]),
    )


def small_layout(z):
    d, half = z.width, z.filt // 2
    def line(row, count=1):
        return (count * d,), [(row + i, 0, 1, d, 0, i * d) for i in range(count)]
    def short(row):
        return (z.filt,), [(row, 0, 1, z.filt, 0, 0)]
    return dict(
        grad_first_gain=line(Row.FIRST_GAIN), grad_first_shift=line(Row.FIRST_SHIFT), grad_input_bias=line(Row.INPUT_BIAS, 3),
        grad_short_kernel=((3, 3 * d), [(Row.SHORT_KERNEL + 3 * i + s, 0, 1, d, i, s * d) for i in range(3) for s in range(3)]),
        grad_short_bias=line(Row.SHORT_BIAS, 3),
        grad_embed_weight=((z.emb, z.filt), [
            (Row.NETWORK, 2 * LANES, half, z.filt, 0, 0), (Row.NETWORK, 3 * LANES, z.emb - half, z.filt, half, 0)]),
        grad_embed_bias=short(Row.EMBED_BIAS),
        grad_inner_weight=((z.filt, z.filt), [
            (Row.NETWORK, 0, half, z.filt, 0, 0), (Row.NETWORK, LANES, half, z.filt, half, 0)]),
        grad_inner_bias=short(Row.INNER_BIAS),
        grad_filter_weight=((z.filt, d), [(Row.FILTER, 0, z.filt, d, 0, 0)]),
        grad_decay_rates=line(Row.DECAY), grad_filter_bias=line(Row.FILTER_BIAS), grad_output_bias=line(Row.OUTPUT_BIAS),
        grad_second_gain=line(Row.SECOND_GAIN), grad_second_shift=line(Row.SECOND_SHIFT),
        grad_up_bias=line(Row.UP_BIAS, z.hidden // d), grad_down_bias=line(Row.DOWN_BIAS),
    )


RUN = 192


def finish_kernel(z, order, pieces, *refs):
    weights, little, names = order
    v = Names(names, refs)
    loads, stores = [], []
    for i, (part, name, row, column, at, rows, columns) in enumerate(pieces):
        source, target = getattr(v, "r_" + part), getattr(v, "l_" + part)
        wide, out = getattr(v, "w_" + name), getattr(v, name)
        there = (pl.ds(row, rows), pl.ds(column, columns))
        loads.append(pltpu.make_async_copy(source.at[pl.ds(at, rows), :], target.at[pl.ds(at, rows), :], v.loads.at[i]))
        stores.append(pltpu.make_async_copy(wide.at[there], out.at[there], v.stores.at[i]))
    for copy in loads:
        copy.start()
    others = [
        pltpu.make_async_copy(v.block_output, v.output, v.others.at[0]),
        pltpu.make_async_copy(v.block_grad_tokens, v.grad_tokens, v.others.at[1]),
    ]
    for copy in others:
        copy.start()
    for i, (part, name, row, column, at, rows, columns) in enumerate(pieces):
        loads[i].wait()
        getattr(v, "w_" + name)[row:row + rows, column:column + columns] = getattr(v, "l_" + part)[at:at + rows, :].astype(F32)
        stores[i].start()
    for name, (shape, moves) in small_layout(z).items():
        out = getattr(v, name)
        for row, column, rows, columns, to_row, to_column in moves:
            value = v.r_small[row:row + rows, column:column + columns]
            if len(shape) == 1:
                out[to_column:to_column + columns] = value.reshape(columns)
            else:
                out[to_row:to_row + rows, to_column:to_column + columns] = value
    for copy in stores + others:
        copy.wait()


def finish(z, results):
    layout, little = finish_layout(z), small_layout(z)
    shapes = part_shapes(z)
    pieces = []
    for name in layout:
        for part, row, column in layout[name][1]:
            rows, columns = shapes[part][0]
            for at in range(0, rows, RUN):
                pieces.append((part, name, row + at, column, at, min(RUN, rows - at), columns))
    any_space, vmem = pl.BlockSpec(memory_space=pl.ANY), pl.BlockSpec(memory_space=pltpu.VMEM)
    parts = [part for part in PARTS if part != PARTS[-1]]
    arguments = dict(("r_" + part, results["r_" + part]) for part in PARTS)
    arguments.update(block_output=results["output"], block_grad_tokens=results["grad_tokens"])
    outs = dict((name, jax.ShapeDtypeStruct(layout[name][0], F32)) for name in layout)
    token_shape = jax.ShapeDtypeStruct((z.tokens, z.width), BF16)
    outs.update(output=token_shape, grad_tokens=token_shape)
    outs.update((name, jax.ShapeDtypeStruct(little[name][0], F32)) for name in little)
    scratch = dict(("l_" + part, pltpu.VMEM(*shapes[part])) for part in parts)
    scratch.update(("w_" + name, pltpu.VMEM(layout[name][0], F32)) for name in layout)
    scratch.update(
        loads=pltpu.SemaphoreType.DMA((len(pieces),)), stores=pltpu.SemaphoreType.DMA((len(pieces),)), others=pltpu.SemaphoreType.DMA((2,))
    )
    names = tuple(arguments) + tuple(outs) + tuple(scratch)
    outputs = pl.pallas_call(
        functools.partial(finish_kernel, z, (tuple(layout), tuple(little), names), pieces),
        out_shape=list(outs.values()),
        in_specs=[any_space] * len(parts) + [vmem, any_space, any_space],
        out_specs=[any_space] * (len(layout) + 2) + [vmem] * len(little),
        scratch_shapes=list(scratch.values()),
        compiler_params=pltpu.CompilerParams(vmem_limit_bytes=58 << 20),
        name="widen_gradients",
    )(*arguments.values())
    return Names(outs, outputs)


def shards(
    n, tokens, doc_lengths, first_gain, first_shift, input_weight, input_bias, short_kernel, short_bias, embed_weight, embed_bias,
    inner_weight, inner_bias, filter_weight, decay_rates, filter_bias, output_weight, output_bias, second_gain, second_shift,
    up_weight, up_bias, down_weight, down_bias, cotangent,
):
    rows, local, width = tokens.shape
    z = Sizes(n, rows, local, width, *embed_weight.shape, up_weight.shape[1])
    z.plans = part_plans(z)
    inputs = dict(
        tokens=tokens.reshape(rows * local, width), doc_lengths=doc_lengths, first_gain=first_gain, first_shift=first_shift,
        input_weight=input_weight, input_bias=input_bias, short_kernel=short_kernel, short_bias=short_bias, embed_weight=embed_weight,
        embed_bias=embed_bias, inner_weight=inner_weight, inner_bias=inner_bias, filter_weight=filter_weight, decay_rates=decay_rates,
        filter_bias=filter_bias, output_weight=output_weight, output_bias=output_bias, second_gain=second_gain,
        second_shift=second_shift, up_weight=up_weight, up_bias=up_bias, down_weight=down_weight, down_bias=down_bias,
        cotangent=cotangent.reshape(rows * local, width),
    )
    o = finish(z, block(z, inputs))
    return (
        o.output.reshape(tokens.shape), o.grad_tokens.reshape(tokens.shape), o.grad_first_gain, o.grad_first_shift, o.grad_input_weight,
        o.grad_input_bias, o.grad_short_kernel, o.grad_short_bias, o.grad_embed_weight, o.grad_embed_bias, o.grad_inner_weight,
        o.grad_inner_bias, o.grad_filter_weight, o.grad_decay_rates, o.grad_filter_bias, o.grad_output_weight, o.grad_output_bias,
        o.grad_second_gain, o.grad_second_shift, o.grad_up_weight, o.grad_up_bias, o.grad_down_weight, o.grad_down_bias,
    )


def solution(mesh):
    split, whole = P(None, "seq", None), P()
    return jax.shard_map(
        functools.partial(shards, mesh.shape["seq"]),
        mesh=mesh,
        in_specs=(split,) + (whole,) * 22 + (split,),
        out_specs=(split, split) + (whole,) * 21,
        check_vma=False,
    )
```

time: 368 us -> 278 us (0.76)
  other arithmetic: 33.9 us -> 0 us
  matrix products: 31.5 us -> 0 us
  local copies, waits for them, and re-layouts: 22.4 us -> 0 us
    dot_general x12 -> x0, matrix products: 31.5 us -> none  [the longest x1 4.45 us: shards(): jnp.einsum('rsf,rsd->fd', hidden, cotangent, preferred_element_type=jnp.f...]
    convert_element_type x7 -> x0, other arithmetic: 19 us -> none  [the longest x4 17.3 us: shards(): v.astype(jnp.float32)]
    slice x21 -> x0, local copies, waits for them, and re-layouts: 13.3 us -> none  [the longest x11 8.73 us: shards(): parts.append(flat[at:at + v.size].reshape(v.shape))]
    reduce_sum x9 -> x0, other arithmetic: 9.59 us -> none  [the longest x1 3.14 us: shards(): grad_input_bias = jnp.sum(grad_proj_low.astype(jnp.float32), axis=(0, 1))]
    pallas_call x3 -> x2, Pallas kernels: 275 us -> 275 us  [the longest x1 248 us: block(): pl.pallas_call(functools.partial(block_kernel, z, order, SCHEDULE), out_s...]
  transfers between devices with their start and end apart: 2 -> 0, of which waited for: 0 -> 0; matrix products, arithmetic and copies ran while one was open for 1% -> 0% of each run, Pallas kernels for 0% -> 0%
where the time goes in v2:
time: 278 us; the launch traced here: 276 us
  Pallas kernels  275 us (99%)
    pallas_call x1, Pallas kernels, block(): pl.pallas_call(functools.partial(block_kernel, z, order, SCHEDULE), out_s...  248 us
    pallas_call x1, Pallas kernels, finish(): pl.pallas_call(functools.partial(finish_kernel, z, (tuple(layout), tuple(...  27.4 us

profile of v2, /device:TPU:0, one launch (start us, length us, event | category | flops | bytes accessed | tf_op | source)
XLA Modules:
  0.0 276.1 jit_solution(12518037357590633110)
XLA Ops:
  0.7 247.8 %hyena_block.1 = (bf16[256,768]{1,0:T(8,128)(2,1)}, bf16[256,768]{1,0:T(8,128)(2,1)}, bf16[1536,768]{1,0:T(8,128)(2,1)}, bf16[768,1536]{1,0:T(8,128)(2,1)}, bf16...) custom-call(bf16[256,768]{1,0:T(8,128)(2,1)} %bitcast.4, ...), custom_call_target="tpu_custom_call" | custom-call | tf_op jit(solution)/shard_map/hyena_block/pallas_call | solution.py:993
  248.5 27.4 %widen_gradients.1 = (f32[3072,768]{1,0:T(8,128)}, f32[768,3072]{1,0:T(8,128)}, f32[768,768]{1,0:T(8,128)}, f32[768,2304]{1,0:T(8,128)}, bf16[256,768]{1,0:T(8,1...) custom-call(bf16[1536,768]{1,0:T(8,128)(2,1)} %get-tuple-element.56., ...), custom_call_target="tpu_custom_call" | custom-call | tf_op jit(solution)/shard_map/widen_gradients/pallas_call | solution.py:1112
